TPU v7x, 32 devices: a whole 2x2x4 slice. The times are simulated.
32 devices in a mesh: batch: 2 (over x), ctx: 16 (over z, y, core).
Axes of the slice: x: 2, y: 2, z: 4, core: 2. Of those that a mesh axis runs over, the one named last changes fastest.
Arguments:
- layer_input: bfloat16 [4, 2, 1536, 768], P('batch', None, 'ctx'), may hold values from -6 to 6
- cotangent: bfloat16 [4, 2, 1536, 768], P('batch', None, 'ctx'), may hold values from -6 to 6
- prefix: int32 [4], P('batch'), may hold values from 153 to 768, as said below
- block_size: int32 [4], P('batch'), may hold values from 4 to 16, as said below
- ln1_gain: bfloat16 [768], P(('batch', 'ctx')), may hold values from 0.5 to 1.5
- ln1_bias: bfloat16 [768], P(('batch', 'ctx')), may hold values from -1.75 to 1.75
- qkv_weight: bfloat16 [768, 2304], P(('batch', 'ctx')), may hold values from -0.21875 to 0.21875
- qkv_bias: bfloat16 [2304], P(('batch', 'ctx')), may hold values from -0.1875 to 0.1875
- out_weight: bfloat16 [768, 768], P(('batch', 'ctx')), may hold values from -0.625 to 0.625
- out_bias: bfloat16 [768], P(('batch', 'ctx')), may hold values from -0.625 to 0.625
- ln2_gain: bfloat16 [768], P(('batch', 'ctx')), may hold values from 0.5 to 1.5
- ln2_bias: bfloat16 [768], P(('batch', 'ctx')), may hold values from -1.75 to 1.75
- up_weight: bfloat16 [768, 3072], P(('batch', 'ctx')), may hold values from -0.21875 to 0.21875
- up_bias: bfloat16 [3072], P(('batch', 'ctx')), may hold values from -1.75 to 1.75
- down_weight: bfloat16 [3072, 768], P(('batch', 'ctx')), may hold values from -0.109375 to 0.109375
- down_bias: bfloat16 [768], P(('batch', 'ctx')), may hold values from -1.75 to 1.75
Outputs:
- block_out: bfloat16 [4, 2, 1536, 768], P('batch', None, 'ctx')
- grad_input: bfloat16 [4, 2, 1536, 768], P('batch', None, 'ctx')
- grad_ln1_gain: float32 [768], P(('batch', 'ctx'))
- grad_ln1_bias: float32 [768], P(('batch', 'ctx'))
- grad_qkv_weight: float32 [768, 2304], P(('batch', 'ctx'))
- grad_qk_bias: float32 [1536], P(('batch', 'ctx'))
- grad_value_bias: float32 [768], P(('batch', 'ctx'))
- grad_out_weight: float32 [768, 768], P(('batch', 'ctx'))
- grad_out_bias: float32 [768], P(('batch', 'ctx'))
- grad_ln2_gain: float32 [768], P(('batch', 'ctx'))
- grad_ln2_bias: float32 [768], P(('batch', 'ctx'))
- grad_up_weight: float32 [768, 3072], P(('batch', 'ctx'))
- grad_up_bias: float32 [3072], P(('batch', 'ctx'))
- grad_down_weight: float32 [3072, 768], P(('batch', 'ctx'))
- grad_down_bias: float32 [768], P(('batch', 'ctx'))
Inputs may be any that keep to these rules, and one draw needn't show every extreme that they name: `prefix`: per sequence, from a tenth to a half of 1536; in every draw some sequence has exactly 153 and some exactly 768. `block_size`: each value is 4, 8 or 16, and all three occur in every draw.
All inputs are finite; a program needn't handle non-finite values.
Results may differ from a plain program's by a relative error of at most 0.019.
Values may be sent and summed in bfloat16 or wider, within the bound.
No kernel may reach another device: no remote copies, remote signals or barrier semaphores. Data moves between devices by JAX's collectives and lax.ppermute only.
A program may use at most 256 MiB of HBM per device.

v0:
```python
import functools

import jax
import jax.numpy as jnp
from jax import lax
from jax.experimental import pallas as pl
from jax.experimental.pallas import tpu as pltpu
from jax.sharding import PartitionSpec as P

HEADS = 12
HEAD_DIM = 64
SCALE = 0.125
NEGATIVE = -1e30
EPSILON = 1e-05
THETA = 10000.0
LANES = 128
BF16 = jnp.bfloat16
F32 = jnp.float32
VMEM_LIMIT = 56 * 1024 * 1024
NT = (((1,), (1,)), ((), ()))
LIGHT = pl.CostEstimate(flops=1, bytes_accessed=1, transcendentals=0)


def swap_halves(tile):
    lane = lax.broadcasted_iota(jnp.int32, tile.shape, 1)
    return jnp.where(lane % 64 < 32, pltpu.roll(tile, LANES - 32, 1), pltpu.roll(tile, 32, 1))


def project_rows(x, gain_ref, bias_ref, w_ref, add_ref, cos_ref, sin_ref, out_ref, unit_ref, start, turned):
    x = x.astype(F32)
    center = x - jnp.mean(x, -1, keepdims=True)
    spread = jnp.mean(center * center, -1, keepdims=True)
    unit = center * lax.rsqrt(spread + EPSILON)
    unit_ref[...] = unit.astype(BF16)
    normed = (unit * gain_ref[...] + bias_ref[...]).astype(BF16)
    cos_tab, sin_tab = cos_ref[...], sin_ref[...]
    total = jnp.dot(normed, w_ref[:, start:], preferred_element_type=F32) + add_ref[:, start:]
    for tile in range(total.shape[1] // LANES):
        part = total[:, tile * LANES : (tile + 1) * LANES]
        if tile * LANES < turned:
            part = part * cos_tab + swap_halves(part) * sin_tab
        out_ref[:, tile * LANES : (tile + 1) * LANES] = part.astype(BF16)


def project_kernel(x_ref, *refs, start, turned):
    project_rows(x_ref[...], *refs, start, turned)


def project_parts_kernel(where_ref, a_ref, b_ref, c_ref, d_ref, *refs, start, turned):
    *refs, rows_ref = refs
    rows = rows_ref.shape[0] // 4
    for index, part in enumerate((a_ref, b_ref, c_ref, d_ref)):
        first = pl.multiple_of(where_ref[1 + index] * rows, rows)
        rows_ref[pl.ds(first, rows), :] = part[0, :rows, :]
    project_rows(rows_ref[...], *refs, start, turned)


def project_parts(where, parts, rows, gain, bias, weight, add, cos_tab, sin_tab, start, turned):
    deep, _, width = parts[0].shape
    columns = weight.shape[1] - start
    block = 4 * rows
    row_map = lambda i, w: (i, 0)
    fixed = lambda i, w: (0, 0)
    spec = pltpu.PrefetchScalarGridSpec(
        num_scalar_prefetch=1,
        grid=(deep,),
        in_specs=[
            pl.BlockSpec((1,) + part.shape[1:], lambda i, w: (lax.rem(w[0] - i + deep, deep), 0, 0)) for part in parts
        ]
        + [
            pl.BlockSpec((1, width), fixed),
            pl.BlockSpec((1, width), fixed),
            pl.BlockSpec(weight.shape, fixed),
            pl.BlockSpec((1, weight.shape[1]), fixed),
            pl.BlockSpec((block, LANES), row_map),
            pl.BlockSpec((block, LANES), row_map),
        ],
        out_specs=[pl.BlockSpec((block, columns), row_map), pl.BlockSpec((block, width), row_map)],
        scratch_shapes=[pltpu.VMEM((block, width), BF16)],
    )
    return pl.pallas_call(
        functools.partial(project_parts_kernel, start=start, turned=turned),
        grid_spec=spec,
        out_shape=[
            jax.ShapeDtypeStruct((deep * block, columns), BF16),
            jax.ShapeDtypeStruct((deep * block, width), BF16),
        ],
        compiler_params=pltpu.CompilerParams(vmem_limit_bytes=VMEM_LIMIT),
        cost_estimate=LIGHT,
        name="project_parts",
    )(where, *parts, gain, bias, weight, add, cos_tab, sin_tab)


def project(x, gain, bias, weight, add, cos_tab, sin_tab, start, turned, block):
    table_blocks = cos_tab.shape[0] // block
    rows, width = x.shape
    columns = weight.shape[1] - start
    row_map = lambda i: (i, 0)
    fixed = lambda i: (0, 0)
    return pl.pallas_call(
        functools.partial(project_kernel, start=start, turned=turned),
        grid=(rows // block,),
        in_specs=[
            pl.BlockSpec((block, width), row_map),
            pl.BlockSpec((1, width), fixed),
            pl.BlockSpec((1, width), fixed),
            pl.BlockSpec(weight.shape, fixed),
            pl.BlockSpec((1, weight.shape[1]), fixed),
            pl.BlockSpec((block, LANES), lambda i: (i % table_blocks, 0)),
            pl.BlockSpec((block, LANES), lambda i: (i % table_blocks, 0)),
        ],
        out_specs=[pl.BlockSpec((block, columns), row_map), pl.BlockSpec((block, width), row_map)],
        out_shape=[jax.ShapeDtypeStruct((rows, columns), BF16), jax.ShapeDtypeStruct((rows, width), BF16)],
        compiler_params=pltpu.CompilerParams(vmem_limit_bytes=VMEM_LIMIT),
        cost_estimate=LIGHT,
        name="project",
    )(x, gain, bias, weight, add, cos_tab, sin_tab)


def place_kernel(where_ref, *refs, rows):
    *sources, out_ref = refs
    deep = sources[0].shape[0]
    for index in range(len(sources) * deep):
        first = pl.multiple_of(where_ref[index] * rows, rows)
        out_ref[pl.ds(first, rows), :] = sources[index // deep][index % deep, :rows, :]


def place(sources, where, rows):
    deep, _, width = sources[0].shape
    blocks = len(sources) * deep
    if rows % 16:
        out = jnp.concatenate([source[:, :rows] for source in sources])
        for index in range(blocks):
            block = sources[index // deep][index % deep, :rows]
            out = lax.dynamic_update_index_in_dim(out, block, where[index], 0)
        return out.reshape(blocks * rows, width)
    spec = pltpu.PrefetchScalarGridSpec(
        num_scalar_prefetch=1,
        grid=(1,),
        in_specs=[pl.BlockSpec(source.shape, lambda i, w: (0, 0, 0)) for source in sources],
        out_specs=pl.BlockSpec((blocks * rows, width), lambda i, w: (0, 0)),
    )
    return pl.pallas_call(
        functools.partial(place_kernel, rows=rows),
        grid_spec=spec,
        out_shape=jax.ShapeDtypeStruct((blocks * rows, width), sources[0].dtype),
        compiler_params=pltpu.CompilerParams(vmem_limit_bytes=VMEM_LIMIT),
        cost_estimate=LIGHT,
        name="place",
    )(where, *sources)


def head_parts(rows, factor):
    rows = rows.astype(F32) * factor
    lane = lax.broadcasted_iota(jnp.int32, rows.shape, 1)
    first = lane < HEAD_DIM
    return (jnp.where(first, rows, 0.0).astype(BF16), jnp.where(first, 0.0, rows).astype(BF16))


def flipped(tile):
    return tile.astype(F32).T.astype(BF16)


def nt_dot(a, b):
    return lax.dot_general(a, b, NT, preferred_element_type=F32)


def sight(scalars_ref, rows):
    prefix, size, first = scalars_ref[0], scalars_ref[1], scalars_ref[2]
    row = lax.broadcasted_iota(jnp.int32, (1, rows), 1)
    noisy = row < rows // 2
    position = first + jnp.where(noisy, row, row - rows // 2)
    near = jnp.floor((position.astype(F32) + 0.5) / size.astype(F32)).astype(jnp.int32) * size
    clean_limit = jnp.where(position < prefix, prefix, near + size)
    limit = jnp.where(noisy, jnp.maximum(near, prefix), clean_limit)
    low = near - first
    return limit, low, jnp.where(noisy, low + size, low)


def own_mask(low, high, noisy_rows):
    at = lax.broadcasted_iota(jnp.int32, (noisy_rows, low.shape[1]), 0)
    return (at >= low) & (at < high)


def attend_kernel(scalars_ref, q_ref, kn_ref, vn_ref, kc_ref, vc_ref, o_ref, log_ref, *, block):
    rows = q_ref.shape[0]
    queries = head_parts(q_ref[...], SCALE)
    limit, low, high = sight(scalars_ref, rows)

    def fold(state, parts):
        values = [flipped(part_values) for _, part_values, _ in parts]
        out = []
        for h in range(2):
            best, total, acc = state[h]
            heads = slice(h * HEAD_DIM, (h + 1) * HEAD_DIM)
            scores = [jnp.where(mask, nt_dot(keys, queries[h]), NEGATIVE) for keys, _, mask in parts]
            tops = [jnp.max(part, 0, keepdims=True) for part in scores]
            new_best = functools.reduce(jnp.maximum, tops, best)
            factor = jnp.exp(best - new_best)
            total = total * factor
            acc = acc * factor
            for part, part_values in zip(scores, values):
                weights = jnp.exp(part - new_best)
                total = total + jnp.sum(weights, 0, keepdims=True)
                acc = acc + jnp.dot(part_values[heads], weights.astype(BF16), preferred_element_type=F32)
            out.append((new_best, total, acc))
        return tuple(out)

    def clean_parts(index):
        parts = []
        for offset in range(0, block, piece):
            first = index * block + offset
            at = lax.broadcasted_iota(jnp.int32, (piece, rows), 0) + first
            if not isinstance(first, int):
                first = pl.multiple_of(first, piece)
            parts.append((kc_ref[pl.ds(first, piece), :], vc_ref[pl.ds(first, piece), :], at < limit))
        return parts

    piece = key_block(block, 512)
    own_part = (kn_ref[...], vn_ref[...], own_mask(low, high, kn_ref.shape[0]))
    start = (
        jnp.full((1, rows), NEGATIVE, F32),
        jnp.zeros((1, rows), F32),
        jnp.zeros((HEAD_DIM, rows), F32),
    )
    if block == kc_ref.shape[0]:
        state = fold((start, start), clean_parts(0) + [own_part])
    else:
        state = lax.fori_loop(0, kc_ref.shape[0] // block, lambda i, state: fold(state, clean_parts(i)), (start, start))
        state = fold(state, [own_part])
    o_ref[...] = jnp.concatenate([acc / total for _, total, acc in state], 0).T.astype(BF16)
    for h in range(2):
        log_ref[0, h : h + 1, :] = state[h][0] + jnp.log(state[h][1])


def attend(scalars, own, s, seqs, clean, block):
    rows = own.shape[0] // seqs
    length = clean.shape[0]
    pairs = own.shape[1] // (3 * LANES)
    spec = pltpu.PrefetchScalarGridSpec(
        num_scalar_prefetch=1,
        grid=(pairs,),
        in_specs=[
            pl.BlockSpec((rows, LANES), lambda p, c: (s, p)),
            pl.BlockSpec((rows // 2, LANES), lambda p, c: (2 * s, pairs + p)),
            pl.BlockSpec((rows // 2, LANES), lambda p, c: (2 * s, 2 * pairs + p)),
            pl.BlockSpec((length, LANES), lambda p, c: (0, p)),
            pl.BlockSpec((length, LANES), lambda p, c: (0, pairs + p)),
        ],
        out_specs=[
            pl.BlockSpec((rows, LANES), lambda p, c: (0, p)),
            pl.BlockSpec((1, 8, rows), lambda p, c: (p, 0, 0)),
        ],
    )
    return pl.pallas_call(
        functools.partial(attend_kernel, block=block),
        grid_spec=spec,
        out_shape=[
            jax.ShapeDtypeStruct((rows, pairs * LANES), BF16),
            jax.ShapeDtypeStruct((pairs, 8, rows), F32),
        ],
        compiler_params=pltpu.CompilerParams(vmem_limit_bytes=VMEM_LIMIT),
        cost_estimate=LIGHT,
        name="attend",
    )(scalars, own, own, own, clean, clean)


def attend_back_kernel(
    scalars_ref, q_ref, kn_ref, vn_ref, kc_ref, vc_ref, o_ref, do_ref, log_ref,
    cos_own_ref, sin_own_ref, cos_ref, sin_ref, dkv_ref, down_ref, sum_ref, *, block
):
    rows = q_ref.shape[0]
    noisy = kn_ref.shape[0]
    width = dkv_ref.shape[1] // 2
    length = kc_ref.shape[0]
    here = pl.multiple_of(pl.program_id(0) * LANES, LANES)
    queries = head_parts(q_ref[...], SCALE)
    grads = head_parts(do_ref[...], 1.0)
    limit, low, high = sight(scalars_ref, rows)
    product = do_ref[...].astype(F32) * o_ref[...].astype(F32)
    lane = lax.broadcasted_iota(jnp.int32, (8, LANES), 1)
    deltas = []
    for h in range(2):
        ones = jnp.where((lane < HEAD_DIM) == (h == 0), 1.0, 0.0)
        deltas.append(
            lax.dot_general(ones, product, NT, precision=lax.Precision.HIGHEST, preferred_element_type=F32)[0:1]
        )

    def fold(dq, keys, values, mask):
        keys_flipped = flipped(keys)
        dk = dv = None
        out = []
        for h in range(2):
            scores = nt_dot(keys, queries[h])
            probs = jnp.where(mask, jnp.exp(scores - log_ref[0, h : h + 1, :]), 0.0)
            inner = nt_dot(values, grads[h])
            slopes = (probs * (inner - deltas[h])).astype(BF16)
            dv_new = jnp.dot(probs.astype(BF16), grads[h], preferred_element_type=F32)
            dk_new = jnp.dot(slopes, queries[h], preferred_element_type=F32)
            dv = dv_new if dv is None else dv + dv_new
            dk = dk_new if dk is None else dk + dk_new
            out.append(
                dq[h]
                + jnp.dot(keys_flipped[h * HEAD_DIM : (h + 1) * HEAD_DIM], slopes, preferred_element_type=F32)
            )
        return tuple(out), dk, dv

    def unturn(grad, cos_tab, sin_tab):
        return grad * cos_tab - swap_halves(grad) * sin_tab

    def step(index, carry):
        dq, sum_k, sum_v = carry
        first = pl.multiple_of(index * block, block)
        where = pl.ds(first, block)
        at = lax.broadcasted_iota(jnp.int32, (block, rows), 0) + index * block
        dq, dk, dv = fold(dq, kc_ref[where, :], vc_ref[where, :], at < limit)
        dk = unturn(dk, cos_ref[where, :], sin_ref[where, :])
        dkv_ref[where, pl.ds(here, LANES)] = dk.astype(BF16)
        dkv_ref[where, pl.ds(width + here, LANES)] = dv.astype(BF16)
        return dq, sum_k + jnp.sum(dk, 0, keepdims=True), sum_v + jnp.sum(dv, 0, keepdims=True)

    zero_q = jnp.zeros((HEAD_DIM, rows), F32)
    zero_sum = jnp.zeros((1, LANES), F32)
    dq, sum_k, sum_v = lax.fori_loop(0, length // block, step, ((zero_q, zero_q), zero_sum, zero_sum))

    dq, dk, dv = fold(dq, kn_ref[...], vn_ref[...], own_mask(low, high, noisy))
    dk = unturn(dk, cos_own_ref[:noisy, :], sin_own_ref[:noisy, :])
    dq = unturn(jnp.concatenate(dq, 0).T * SCALE, cos_own_ref[...], sin_own_ref[...])
    zeros = jnp.zeros((rows - noisy, LANES), BF16)
    for part, grad in enumerate((dq, dk, dv)):
        down_ref[: grad.shape[0], pl.ds(part * width + here, LANES)] = grad.astype(BF16)
        if part > 0:
            down_ref[noisy:, pl.ds(part * width + here, LANES)] = zeros
    sums = (
        jnp.sum(dq, 0, keepdims=True),
        sum_k + jnp.sum(dk, 0, keepdims=True),
        sum_v + jnp.sum(dv, 0, keepdims=True),
    )
    for part in range(3):
        sum_ref[:, pl.ds(part * width + here, LANES)] = jnp.broadcast_to(sums[part], (8, LANES))


def attend_back(scalars, own, s, seqs, clean, attn, grad, log_total, cos_own, sin_own, cos_tab, sin_tab, block):
    rows = own.shape[0] // seqs
    length, both = clean.shape
    pairs = own.shape[1] // (3 * LANES)
    spec = pltpu.PrefetchScalarGridSpec(
        num_scalar_prefetch=1,
        grid=(pairs,),
        in_specs=[
            pl.BlockSpec((rows, LANES), lambda p, c: (s, p)),
            pl.BlockSpec((rows // 2, LANES), lambda p, c: (2 * s, pairs + p)),
            pl.BlockSpec((rows // 2, LANES), lambda p, c: (2 * s, 2 * pairs + p)),
            pl.BlockSpec((length, LANES), lambda p, c: (0, p)),
            pl.BlockSpec((length, LANES), lambda p, c: (0, pairs + p)),
            pl.BlockSpec((rows, LANES), lambda p, c: (0, p)),
            pl.BlockSpec((rows, LANES), lambda p, c: (0, p)),
            pl.BlockSpec((1, 8, rows), lambda p, c: (p, 0, 0)),
            pl.BlockSpec((rows, LANES), lambda p, c: (0, 0)),
            pl.BlockSpec((rows, LANES), lambda p, c: (0, 0)),
            pl.BlockSpec((length, LANES), lambda p, c: (0, 0)),
            pl.BlockSpec((length, LANES), lambda p, c: (0, 0)),
        ],
        out_specs=[
            pl.BlockSpec((length, both), lambda p, c: (0, 0)),
            pl.BlockSpec((rows, own.shape[1]), lambda p, c: (0, 0)),
            pl.BlockSpec((8, own.shape[1]), lambda p, c: (0, 0)),
        ],
    )
    return pl.pallas_call(
        functools.partial(attend_back_kernel, block=block),
        grid_spec=spec,
        out_shape=[
            jax.ShapeDtypeStruct((length, both), BF16),
            jax.ShapeDtypeStruct((rows, own.shape[1]), BF16),
            jax.ShapeDtypeStruct((8, own.shape[1]), F32),
        ],
        compiler_params=pltpu.CompilerParams(vmem_limit_bytes=VMEM_LIMIT),
        cost_estimate=LIGHT,
        name="attend_back",
    )(scalars, own, own, own, clean, clean, attn, grad, log_total, cos_own, sin_own, cos_tab, sin_tab)


def feed_forward_kernel(
    core_ref, attn_ref, x_ref, top_ref, up_ref, down_ref, out_ref, vec_ref,
    block_out_ref, hidden_grad_ref, attn_grad_ref, weights_ref, mine_ref, theirs_ref,
    hidden, unit, inverse, normed, normed_flipped, lowered, grad_normed,
    up_grads, join_grads, down_grads, out_grads, vec_grads, sums, up_sems, join_sems, down_sems, last_sems,
    *, pairs, joined
):
    chunk = pl.program_id(0)
    chunks = pl.num_programs(0)
    width = x_ref.shape[1]

    @pl.when(chunk == 0)
    def _():
        value = (
            x_ref[...].astype(F32)
            + jnp.dot(attn_ref[...], out_ref[...], preferred_element_type=F32)
            + vec_ref[0:1, :]
        )
        hidden[...] = value
        center = value - jnp.mean(value, -1, keepdims=True)
        scale = lax.rsqrt(jnp.mean(center * center, -1, keepdims=True) + EPSILON)
        inverse[...] = scale
        unit[...] = center * scale
        scaled = unit[...] * vec_ref[1:2, :] + vec_ref[2:3, :]
        normed[...] = scaled.astype(BF16)
        normed_flipped[...] = scaled.T.astype(BF16)
        lowered[...] = jnp.zeros_like(lowered)
        grad_normed[...] = jnp.zeros_like(grad_normed)
        sums[...] = jnp.zeros_like(sums)

    upper = jnp.dot(normed[...], up_ref[...], preferred_element_type=F32) + vec_ref[pl.ds(4 + chunk, 1), :]
    grad_activ = nt_dot(top_ref[...], down_ref[...])
    square = upper * upper
    half = 0.5 + 0.5 * jnp.tanh(upper * (0.7978845608028654 + 0.035677408136300125 * square))
    activ = upper * half
    slope = half + activ * (1.0 - half) * (1.5957691216057308 + 0.21406444881780075 * square)
    grad_upper = grad_activ * slope
    grad_low = grad_upper.astype(BF16)
    sums[pl.ds(4 + chunk, 1), :] = jnp.sum(grad_upper, 0, keepdims=True)
    lowered[...] += jnp.dot(activ.astype(BF16), down_ref[...], preferred_element_type=F32)
    grad_normed[...] += nt_dot(grad_low, up_ref[...])
    up_grads[chunk] = jnp.dot(normed_flipped[...], grad_low, preferred_element_type=F32).astype(BF16)
    down_grad = jnp.dot(activ.T.astype(BF16), top_ref[...], preferred_element_type=F32).astype(BF16)
    shard = width // (2 * pairs)

    @pl.when(chunk < joined)
    def _():
        join_grads[chunk] = down_grad

    @pl.when(chunk >= joined)
    def _():
        for pair in range(pairs):
            for core in range(2):
                first = (2 * pair + core) * shard
                down_grads[chunk - joined, core, pair * shard : (pair + 1) * shard, :] = down_grad[first : first + shard]

    def copy_up(index):
        columns = pl.ds(pl.multiple_of(index * width, width), width)
        return pltpu.make_async_copy(up_grads.at[index], weights_ref.at[:, columns], up_sems.at[index])

    def copy_join(index):
        columns = pl.ds(pl.multiple_of((chunks + index) * width, width), width)
        return pltpu.make_async_copy(join_grads.at[index], weights_ref.at[:, columns], join_sems.at[index])

    def copy_down(index):
        columns = pl.ds(pl.multiple_of(index * width, width), width)
        core = core_ref[0]
        return (
            pltpu.make_async_copy(down_grads.at[index, core], mine_ref.at[:, columns], down_sems.at[0, index]),
            pltpu.make_async_copy(down_grads.at[index, 1 - core], theirs_ref.at[:, columns], down_sems.at[1, index]),
        )

    copy_up(chunk).start()

    @pl.when(chunk < joined)
    def _():
        copy_join(chunk).start()

    @pl.when(chunk >= joined)
    def _():
        for copy in copy_down(chunk - joined):
            copy.start()

    @pl.when(chunk == chunks - 1)
    def _():
        top = top_ref[...].astype(F32)
        block_out_ref[...] = (hidden[...] + lowered[...] + vec_ref[3:4, :]).astype(BF16)
        grad = grad_normed[...]
        rows_unit = unit[...]
        sums[1:2, :] = jnp.sum(grad * rows_unit, 0, keepdims=True)
        sums[2:3, :] = jnp.sum(grad, 0, keepdims=True)
        sums[3:4, :] = jnp.sum(top, 0, keepdims=True)
        grad = grad * vec_ref[1:2, :]
        grad = inverse[...] * (
            grad - jnp.mean(grad, -1, keepdims=True) - rows_unit * jnp.mean(grad * rows_unit, -1, keepdims=True)
        )
        grad = top + grad
        hidden_grad_ref[...] = grad
        sums[0:1, :] = jnp.sum(grad, 0, keepdims=True)
        low = grad.astype(BF16)
        attn_grad_ref[...] = nt_dot(low, out_ref[...]).astype(BF16)
        out_grads[...] = jnp.dot(
            attn_ref[...].astype(F32).T.astype(BF16), low, preferred_element_type=F32
        ).astype(BF16)
        vec_grads[...] = sums[...].T.astype(BF16)
        first = (chunks + joined) * width
        copies = [
            pltpu.make_async_copy(out_grads, weights_ref.at[:, pl.ds(first, width)], last_sems.at[0]),
            pltpu.make_async_copy(vec_grads, weights_ref.at[:, pl.ds(first + width, LANES)], last_sems.at[1]),
        ]
        for copy in copies:
            copy.start()
        for index in range(up_grads.shape[0]):
            copy_up(index).wait()
        for index in range(joined):
            copy_join(index).wait()
        for index in range(down_grads.shape[0]):
            for copy in copy_down(index):
                copy.wait()
        for copy in copies:
            copy.wait()


def feed_forward(core, attn, x, top, weights, vectors, chunks, pairs, joined):
    rows, width = x.shape
    apart = chunks - joined
    fixed = lambda b, c: (0, 0)
    whole = pl.BlockSpec((rows, width), fixed)
    spec = pltpu.PrefetchScalarGridSpec(
        num_scalar_prefetch=1,
        grid=(chunks,),
        in_specs=[
            whole,
            whole,
            whole,
            pl.BlockSpec((width, width), lambda b, c: (0, b)),
            pl.BlockSpec((width, width), lambda b, c: (0, chunks + b)),
            pl.BlockSpec((width, width), lambda b, c: (0, 2 * chunks)),
            pl.BlockSpec(vectors.shape, fixed),
        ],
        out_specs=[whole, whole, whole] + [pl.BlockSpec(memory_space=pl.ANY)] * 3,
        scratch_shapes=[
            pltpu.VMEM((rows, width), F32),
            pltpu.VMEM((rows, width), F32),
            pltpu.VMEM((rows, 1), F32),
            pltpu.VMEM((rows, width), BF16),
            pltpu.VMEM((width, rows), BF16),
            pltpu.VMEM((rows, width), F32),
            pltpu.VMEM((rows, width), F32),
            pltpu.VMEM((chunks, width, width), BF16),
            pltpu.VMEM((joined, width, width), BF16),
            pltpu.VMEM((apart, 2, width // 2, width), BF16),
            pltpu.VMEM((width, width), BF16),
            pltpu.VMEM((width, LANES), BF16),
            pltpu.VMEM((LANES, width), F32),
            pltpu.SemaphoreType.DMA((chunks,)),
            pltpu.SemaphoreType.DMA((joined,)),
            pltpu.SemaphoreType.DMA((2, apart)),
            pltpu.SemaphoreType.DMA((2,)),
        ],
    )
    return pl.pallas_call(
        functools.partial(feed_forward_kernel, pairs=pairs, joined=joined),
        grid_spec=spec,
        out_shape=[
            jax.ShapeDtypeStruct((rows, width), BF16),
            jax.ShapeDtypeStruct((rows, width), F32),
            jax.ShapeDtypeStruct((rows, width), BF16),
            jax.ShapeDtypeStruct((width, weights.shape[1] - apart * width), BF16),
            jax.ShapeDtypeStruct((width // 2, apart * width), BF16),
            jax.ShapeDtypeStruct((width // 2, apart * width), BF16),
        ],
        compiler_params=pltpu.CompilerParams(vmem_limit_bytes=VMEM_LIMIT),
        cost_estimate=LIGHT,
        name="feed_forward",
    )(core.reshape(1), attn, x, top, weights, weights, weights, vectors)


def after(value, *others):
    return lax.optimization_barrier((value,) + others)[0]


def pick(array, index, axis=0):
    return lax.dynamic_index_in_dim(array, index, axis, keepdims=False)


def ordered(flag, own, other, axis):
    return jnp.stack([jnp.where(flag == 0, own, other), jnp.where(flag == 0, other, own)], axis)


class Links:
    def __init__(self):
        self.count = lax.axis_size("ctx")
        self.deep = self.count // 4
        at = lax.axis_index("ctx")
        self.x = lax.axis_index("batch")
        self.core = at % 2
        self.y = (at // 2) % 2
        self.z = at // 4
        self.chip = at // 2

    def over_core(self, array):
        return lax.ppermute(array, "ctx", [(i, i ^ 1) for i in range(self.count)])

    def over_y(self, array):
        return lax.ppermute(array, "ctx", [(i, i ^ 2) for i in range(self.count)])

    def over_x(self, array):
        return lax.ppermute(array, "batch", [(0, 1), (1, 0)])

    def along_z(self, array, hop):
        count = self.count
        return lax.ppermute(array, "ctx", [(i, (i + 4 * hop) % count) for i in range(count)])

    def around_z(self, piece):
        return [self.along_z(piece, hop) for hop in range(1, self.deep)]

    def column(self, piece, others):
        deep = self.deep
        whole = jnp.broadcast_to(piece[None], (deep,) + piece.shape)
        for hop, other in enumerate(others, 1):
            whole = lax.dynamic_update_index_in_dim(whole, other, (self.z - hop) % deep, 0)
        return whole

    def swap_z(self, parts):
        return [self.along_z(pick(parts, (self.z + hop) % self.deep), hop) for hop in range(1, self.deep)]

    def sum_z(self, parts, others):
        total = pick(parts, self.z).astype(F32)
        for other in others:
            total = total + other.astype(F32)
        return total


def unit_rows(values):
    center = values - jnp.mean(values, -1, keepdims=True)
    spread = jnp.mean(center * center, -1, keepdims=True)
    inverse = lax.rsqrt(spread + EPSILON)
    return center * inverse, inverse


def unit_back(grad, unit, inverse):
    return inverse * (
        grad - jnp.mean(grad, -1, keepdims=True) - unit * jnp.mean(grad * unit, -1, keepdims=True)
    )


def rotary_tables(positions):
    half_dim = HEAD_DIM // 2
    inverse = 1.0 / THETA ** (jnp.arange(half_dim, dtype=F32) / half_dim)
    angles = positions.astype(F32)[:, None] * jnp.tile(inverse, LANES // half_dim)[None, :]
    sign = jnp.where(jnp.arange(LANES) % HEAD_DIM < half_dim, -1.0, 1.0)
    return jnp.cos(angles), jnp.sin(angles) * sign[None, :]


def key_block(length, limit):
    sizes = [size for size in range(16, limit + 1, 16) if length % size == 0]
    return sizes[-1] if sizes else length


def row_block(rows):
    for block in (512, 384, 256, 128, 64, 32, 16):
        if rows % block == 0:
            return block
    return rows


def dot(a, b):
    return jnp.dot(a, b, preferred_element_type=F32)


def dot_left(a, b):
    return lax.dot_general(a, b, (((0,), (0,)), ((), ())), preferred_element_type=F32)


def on_device(
    layer_input, cotangent, prefix, block_size, ln1_gain, ln1_bias, qkv_weight, qkv_bias, out_weight, out_bias,
    ln2_gain, ln2_bias, up_weight, up_bias, down_weight, down_bias,
):
    links = Links()
    core = links.core
    seqs, _, pos_dev, width = layer_input.shape
    devices = 2 * links.count
    length = links.count * pos_dev
    half = width // 2
    rows = 4 * pos_dev
    shard = ln1_gain.shape[0]
    hidden_shard = up_bias.shape[0]

    split = qkv_weight.reshape(shard, 3, 2, half)
    vec_one = jnp.concatenate([ln1_gain, ln1_bias, qkv_bias])
    vec_one = ordered(core, vec_one, links.over_core(vec_one), 0).reshape(1, -1)
    vec_one = jnp.pad(vec_one, ((0, 7), (0, width - vec_one.shape[1])))
    qkv_piece = ordered(core, pick(split, core, 2), links.over_core(pick(split, 1 - core, 2)), 0)
    qkv_piece = qkv_piece.reshape(2 * shard, 3 * half)
    cos_tab, sin_tab = rotary_tables(after(jnp.arange(length, dtype=jnp.int32), qkv_piece))
    first_pos = links.chip * 2 * pos_dev
    cos_own = jnp.tile(lax.dynamic_slice_in_dim(cos_tab, first_pos, 2 * pos_dev, 0), (2, 1))
    sin_own = jnp.tile(lax.dynamic_slice_in_dim(sin_tab, first_pos, 2 * pos_dev, 0), (2, 1))
    block = key_block(length, 1536)
    scalars = [jnp.stack([prefix[s], block_size[s], first_pos]) for s in range(seqs)]
    qkv_others = links.around_z(qkv_piece)
    inputs_got = links.over_core(layer_input)
    qkv_column = jnp.stack([qkv_piece] + qkv_others)
    qkv_got = links.over_y(qkv_column)
    qkv_far = links.over_x(qkv_column)
    clean_piece = jnp.concatenate([layer_input[0, 1], vec_one])
    clean_piece = after(clean_piece, cos_tab, sin_tab, inputs_got, *qkv_others)
    clean_others = links.around_z(clean_piece)
    gate = (qkv_got, qkv_far) + tuple(clean_others)
    weights_gate = gate
    qkv_last = links.over_x(after(qkv_got, *gate))
    hops = jnp.arange(links.deep, dtype=jnp.int32)
    levels = (links.z - hops) % links.deep
    arrived = []
    for s in range(seqs):
        column = after(jnp.stack([clean_piece] + clean_others), *gate)
        got = links.over_y(column)
        gate = (got,)
        if s + 1 < seqs:
            clean_piece = after(layer_input[s + 1, 1], column)
            clean_others = links.around_z(clean_piece)
            gate = gate + tuple(clean_others)
        if s == 0:
            vec_near = jnp.stack([column[:, pos_dev], got[:, pos_dev]])
            vec_far = links.over_x(after(vec_near, *gate[1:]))
            gate = gate + (qkv_last,)
        arrived.append((column, got, links.over_core(column)))
    where = jnp.concatenate(
        [(x * links.deep + levels) * 2 + y for x in (links.x, 1 - links.x) for y in (links.y, 1 - links.y)]
    )
    qkv_mat = place([qkv_column, qkv_got, qkv_far, qkv_last], where, 2 * shard)
    vec_one = jnp.concatenate([vec_near, vec_far]).reshape(where.shape[0], width).astype(F32)
    turn = (where[None, :] == jnp.arange(where.shape[0], dtype=jnp.int32)[:, None]).astype(F32)
    vec_one = jnp.dot(turn, vec_one[:, : 2 * (2 * shard + qkv_bias.shape[0])], precision=lax.Precision.HIGHEST)
    vec_one = vec_one.reshape(devices, -1)
    gain_one = vec_one[:, :shard].reshape(1, width)
    bias_one = vec_one[:, shard : 2 * shard].reshape(1, width)
    qkv_add = pick(vec_one[:, 2 * shard :].reshape(3, 2, half), core, 1).reshape(1, 3 * half)

    folds = hidden_shard // shard
    up_piece = up_weight.reshape(shard, devices, folds, shard).transpose(0, 2, 1, 3).reshape(shard, -1)
    down_piece = down_weight.reshape(folds, shard, width).transpose(1, 0, 2).reshape(shard, -1)
    vec_piece = jnp.stack(
        [out_bias, ln2_gain, ln2_bias, down_bias] + [up_bias[i * shard : (i + 1) * shard] for i in range(folds)], 1
    )
    vec_piece = jnp.pad(vec_piece, ((0, 0), (0, LANES - vec_piece.shape[1])))
    packed = after(jnp.concatenate([up_piece, down_piece, out_weight, vec_piece], 1), *weights_gate)
    weights = lax.all_gather(packed, ("batch", "ctx"), axis=0, tiled=True)
    vectors = weights[:, -LANES:].T[: 4 + folds].astype(F32)

    inputs_pair = ordered(core, layer_input, inputs_got, 2).reshape(seqs, rows, width)

    own_qkv, own_unit = project(
        inputs_pair.reshape(seqs * rows, width), gain_one, bias_one, qkv_mat, qkv_add,
        cos_own, sin_own, 0, width, row_block(rows),
    )
    clean_kv, clean_unit, attn_list, log_list = ([] for _ in range(4))
    for s in range(seqs):
        column, got, column_far = arrived[s]
        got = after(got, *([clean_kv[-1]] if s else [own_qkv]))
        where = jnp.stack([links.z] + [y * 2 + c for c in (core, 1 - core) for y in (links.y, 1 - links.y)])
        clean, all_unit = project_parts(
            where, [column, got, column_far, links.over_core(got)], pos_dev,
            gain_one, bias_one, qkv_mat, qkv_add, cos_tab, sin_tab, half, half,
        )
        attn, log_total = attend(scalars[s], own_qkv, s, seqs, clean, block)
        for kept, value in zip(
            (clean_kv, clean_unit, attn_list, log_list),
            (clean, all_unit, attn, log_total),
        ):
            kept.append(value)

    attn_rows = jnp.stack(attn_list).reshape(seqs, 2, 2, pos_dev, half)
    attn_got = links.over_core(pick(attn_rows, 1 - core, 2))
    attn_low = ordered(core, pick(attn_rows, core, 2), attn_got, 3).reshape(-1, width)
    flat_inputs = layer_input.reshape(-1, width)
    joined = folds * 3 // 4
    apart = folds - joined
    output, grad_hidden, grad_attn, weight_grads, down_mine, down_theirs = feed_forward(
        core, attn_low, flat_inputs, cotangent.reshape(-1, width), weights, vectors, folds, links.count, joined
    )
    output = output.reshape(layer_input.shape)
    packed = lax.psum_scatter(weight_grads, ("batch", "ctx"), scatter_dimension=0, tiled=True)
    down_got = links.over_core(down_theirs)
    down_part = (down_mine.astype(F32) + down_got.astype(F32)).astype(BF16)
    down_part = down_part.reshape(2, links.deep, 2, shard * apart, width)
    down_sent = pick(down_part, 1 - links.x)
    down_got = links.over_x(down_sent)

    grad_split = grad_attn.reshape(-1, 2, half)
    grad_got = links.over_core(pick(grad_split, 1 - core, 1))
    grad_rows = ordered(
        core,
        pick(grad_split, core, 1).reshape(seqs, 2, pos_dev, half),
        grad_got.reshape(seqs, 2, pos_dev, half),
        2,
    ).reshape(seqs, rows, half)
    kv_mat = qkv_mat[:, half:]
    own_unit = own_unit.reshape(seqs, rows, width)
    unit_part = jnp.zeros((width, 3 * half), F32)
    kv_part = jnp.zeros((width, 2 * half), F32)
    column_sums = 0.0
    waiting, gate = [], ()
    for s in range(seqs):
        clean_grad, own_grad, sums = attend_back(
            scalars[s], own_qkv, s, seqs, clean_kv[s], attn_list[s], after(grad_rows[s], *gate),
            log_list[s], cos_own, sin_own, cos_tab, sin_tab, block,
        )
        spread = lax.dot_general(clean_grad, kv_mat, NT, preferred_element_type=F32).astype(BF16)
        local = lax.dot_general(own_grad, qkv_mat, NT, preferred_element_type=F32).astype(BF16)
        spread = spread.reshape(2 * links.deep, 2, pos_dev, width)
        local = local.reshape(2, 2, pos_dev, width)
        theirs = jnp.concatenate([pick(spread, 1 - core, 1), pick(local, 1 - core, 1)])
        got = links.over_core(theirs)
        gate = (theirs,)
        if s == seqs - 1:
            down_got = after(down_got, own_grad)
            down_part = (pick(down_part, links.x).astype(F32) + down_got.astype(F32)).astype(BF16)
            down_sent = pick(down_part, 1 - links.y, 1)
            down_got = links.over_y(down_sent)
            gate = (theirs, down_sent)
        unit_part = unit_part + dot_left(own_unit[s], after(own_grad, *gate))
        kv_part = kv_part + dot_left(clean_unit[s], after(clean_grad, *gate))
        column_sums = column_sums + sums[0]
        if s == seqs - 1:
            qkv_part = (unit_part + jnp.pad(kv_part, ((0, 0), (half, 0)))).astype(BF16)
            qkv_part = qkv_part.reshape(2, links.deep, 2, 2 * shard, 3 * half)
            far_part = pick(qkv_part, 1 - links.x)
            qkv_far = links.over_x(far_part)
        mine = pick(spread, core, 1).astype(F32) + got[: 2 * links.deep].astype(F32)
        mine = mine.astype(BF16).reshape(links.deep, 2, pos_dev, width)
        local = pick(local, core, 1).astype(F32) + got[2 * links.deep :].astype(F32)
        if s == seqs - 1:
            below = jnp.pad(column_sums, (0, 8 * width - 3 * half)).astype(BF16).reshape(1, 1, 8, width)
            mine = jnp.concatenate([mine, jnp.broadcast_to(below, (links.deep, 2, 8, width))], 2)
        theirs = pick(mine, 1 - links.y, 1)
        row_got = links.over_y(theirs)
        waiting.append((mine, local, row_got))
        gate = (theirs, down_sent)
    down_part = pick(after(down_part, far_part), links.y, 1).astype(F32)
    down_part = (down_part + down_got.astype(F32)).astype(BF16)
    summed = []
    for mine, _, row_got in waiting:
        mine = (pick(mine, links.y, 1).astype(F32) + after(row_got, far_part).astype(F32)).astype(BF16)
        summed.append(mine)
    first = jnp.concatenate(summed[:-1] + [down_part], 1)
    first_others = links.swap_z(first)
    others = links.swap_z(summed[-1])
    total = links.sum_z(summed[-1], others)
    first_others = after(tuple(first_others), summed[-1])
    first = links.sum_z(first, first_others)
    own_rows = [
        jnp.stack([local[0], local[1] + (first[s * pos_dev : (s + 1) * pos_dev] if s < seqs - 1 else total[:pos_dev])])
        for s, (_, local, _) in enumerate(waiting)
    ]
    down_sum = first[(seqs - 1) * pos_dev :]
    column_sums = total[pos_dev:].reshape(-1)[: 3 * half].reshape(3, half)
    column_sums = column_sums + links.over_x(column_sums)
    column_sums = ordered(core, column_sums, links.over_core(column_sums), 1).reshape(3 * width)

    grad_normed_one = jnp.stack(own_rows).reshape(-1, width)
    unit_one, inverse_one = unit_rows(after(flat_inputs, far_part).astype(F32))
    grad_input = grad_hidden + unit_back(grad_normed_one * gain_one, unit_one, inverse_one)
    grad_input = grad_input.astype(BF16).reshape(layer_input.shape)

    qkv_part = (pick(after(qkv_part, packed), links.x).astype(F32) + qkv_far.astype(F32)).astype(BF16)
    qkv_far = links.over_y(after(pick(qkv_part, 1 - links.y, 1), waiting[-1][2]))
    qkv_part = (pick(qkv_part, links.y, 1).astype(F32) + qkv_far.astype(F32)).astype(BF16)
    qkv_part = after(qkv_part, summed[-1])
    qkv_sum = links.sum_z(qkv_part, links.swap_z(qkv_part)).reshape(2, shard, 3, half)
    qkv_got = links.over_core(pick(qkv_sum, 1 - core))
    qkv_sum = ordered(core, pick(qkv_sum, core), qkv_got, 2).reshape(shard, 3 * width)
    grad_qkv = ln1_gain.astype(F32)[:, None] * qkv_sum + ln1_bias.astype(F32)[:, None] * column_sums[None, :]
    own_weight = qkv_weight.astype(F32)
    grad_gain_one = jnp.sum(own_weight * qkv_sum, -1)
    grad_bias_one = jnp.sum(own_weight * column_sums[None, :], -1)
    device = links.x * links.count + lax.axis_index("ctx")
    grad_qk_bias = lax.dynamic_slice_in_dim(column_sums[: 2 * width], device * 2 * shard, 2 * shard, 0)
    grad_value_bias = lax.dynamic_slice_in_dim(column_sums[2 * width :], device * shard, shard, 0)

    hidden_width = devices * hidden_shard
    packed = packed.astype(F32)
    grad_up = packed[:, :hidden_width].reshape(shard, folds, devices, shard).transpose(0, 2, 1, 3)
    grad_up = grad_up.reshape(shard, hidden_width)
    first_down = packed[:, hidden_width : hidden_width + joined * width].reshape(shard, joined, width)
    grad_down = jnp.concatenate([first_down, down_sum.reshape(shard, apart, width)], 1)
    grad_down = grad_down.transpose(1, 0, 2).reshape(hidden_shard, width)
    grad_out = packed[:, hidden_width + joined * width : -LANES]
    late = packed[:, -LANES:].T

    return (
        output, grad_input, grad_gain_one, grad_bias_one, grad_qkv, grad_qk_bias, grad_value_bias, grad_out,
        late[0], late[1], late[2], grad_up, late[4 : 4 + folds].reshape(-1), grad_down, late[3],
    )


def solution(mesh):
    every = P(("batch", "ctx"))
    matrix = P(("batch", "ctx"), None)
    acts = P("batch", None, "ctx", None)
    return jax.shard_map(
        on_device,
        mesh=mesh,
        in_specs=(
            acts, acts, P("batch"), P("batch"), every, every, matrix, every, matrix, every, every, every, matrix,
            every, matrix, every,
        ),
        out_specs=(
            acts, acts, every, every, matrix, every, every, matrix, every, every, every, matrix, every, matrix, every,
        ),
        check_vma=False,
    )
```

profile of v0, /device:TPU:0, one launch (start us, length us, event | category | flops | bytes accessed | tf_op | source)
XLA Modules:
  0.0 367.4 jit_solution(2937611436994412627)
XLA Ops:
  16.7 4.7 %collective-permute-start.5 = (bf16[48,1152]{1,0:T(8,128)(2,1)}, bf16[48,1152]{1,0:T(8,128)(2,1)S(1)}, u32[]{:S(2)}, u32[]{:S(2)}) collective-permute-start(bf16[48,1152]{1,0:T(8,128)(2,1)} %bitcast.141), channel_id=1, source_target_pairs={{0,12},{1,13},{2,14},{3,15},{4,0},{5,1},{6,2},{7,3},{8,4},{9,5},{1... | collective-permute-start | bytes 331784 | tf_op jit(solution)/shard_map/ppermute | solution.py:596
  22.4 2.8 fusion.20
  25.3 6.9 %collective-permute-done.4 = bf16[48,1152]{1,0:T(8,128)(2,1)S(1)} collective-permute-done((bf16[48,1152]{1,0:T(8,128)(2,1)}, bf16[48,1152]{1,0:T(8,128)(2,1)S(1)}, u32[]{:S(2)}, u32[]{:S(2)}) %collective-permute-start.4) | collective-permute-done | bytes 110624 | tf_op jit(solution)/shard_map/ppermute | solution.py:596
  42.6 3.3 collective-permute-done.10.refs_2_
  47.1 5.4 %collective-permute-done.7 = bf16[104,768]{1,0:T(8,128)(2,1)} collective-permute-done((bf16[104,768]{1,0:T(8,128)(2,1)S(1)}, bf16[104,768]{1,0:T(8,128)(2,1)}, u32[]{:S(2)}, u32[]{:S(2)}) %collective-permute-start.7) | collective-permute-done | bytes 159776 | tf_op jit(solution)/shard_map/ppermute | solution.py:596
  56.4 2.1 collective-permute-start.12
  60.3 10.2 %collective-permute-done.11.b_ref = bf16[4,104,768]{2,1,0:T(8,128)(2,1)} collective-permute-done((bf16[4,104,768]{2,1,0:T(8,128)(2,1)S(1)}, bf16[4,104,768]{2,1,0:T(8,128)(2,1)}, u32[]{:S(2)}, u32[]{:S(2)}) %collective-permute-start.11) | collective-permute-done | bytes 639008 | tf_op jit(solution)/shard_map/ppermute | solution.py:589
  71.4 4.8 %collective-permute-done.13 = bf16[96,768]{1,0:T(8,128)(2,1)S(1)} collective-permute-done((bf16[96,768]{1,0:T(8,128)(2,1)S(1)}, bf16[96,768]{1,0:T(8,128)(2,1)S(1)}, u32[]{:S(2)}, u32[]{:S(2)}) %collective-permute-start.13) | collective-permute-done | bytes 147488 | tf_op jit(solution)/shard_map/ppermute | solution.py:596
  78.4 3.4 place.1.refs_2_
  85.7 5.3 %project.1 = (bf16[768,1152]{1,0:T(8,128)(2,1)}, bf16[768,768]{1,0:T(8,128)(2,1)}) custom-call(bf16[768,768]{1,0:T(8,128)(2,1)} %bitcast.273, f32[1,768]{1,0:T(1,128)} %reshape.304.refs_0_, f32[1,768]{1,0:T(1,128)} %reshape.305.refs_1_, bf16[768,1152]{1,0:T(8,128)(2,1)} %place.1.refs_2_, f32[1,1152]{1,0:T(1,128)} %bitcast.321, f32[384,128]{1,0:T(8,128)} %bitcast.280, ...), custom_call_target="tpu_custom_call" | custom-call | flops 1 | bytes 1 | tf_op jit(solution)/shard_map/project/pallas_call | solution.py:100
  95.5 8.4 %project_parts.2 = (bf16[1536,768]{1,0:T(8,128)(2,1)}, bf16[1536,768]{1,0:T(8,128)(2,1)}) custom-call(s32[5]{0:T(128)} %stack.221.where_ref, bf16[4,104,768]{2,1,0:T(8,128)(2,1)} %copy-done.11, bf16[4,104,768]{2,1,0:T(8,128)(2,1)} %collective-permute-done.11.b_ref, bf16[4,104,768]{2,1,0:T(8,128)(2,1)} %copy-done.32, bf16[4,104,768]{2,1,0:T(8,128)(2,1)} %copy-done.33, ...), custom_call_target="tpu_custom_call" | custom-call | flops 1 | bytes 1 | tf_op jit(solution)/shard_map/project_parts/pallas_call | solution.py:81
  103.8 3.0 collective-permute-done.19.b_ref
  111.3 10.8 %attend.2 = (bf16[384,384]{1,0:T(8,128)(2,1)}, f32[3,8,384]{2,1,0:T(8,128)}) custom-call(s32[3]{0:T(128)} %add_add_fusion.scalars_ref, bf16[768,1152]{1,0:T(8,128)(2,1)} %get-tuple-element.69.q_ref.kn_ref.vn_ref, bf16[768,1152]{1,0:T(8,128)(2,1)} %get-tuple-element.69.q_ref.kn_ref.vn_ref, bf16[768,1152]{1,0:T(8,128)(2,1)} %get-tuple-element.69.q_ref.kn_ref.vn_ref, ...), custom_call_target="tpu_custom_call" | custom-call | flops 1 | bytes 1 | tf_op jit(solution)/shard_map/attend/pallas_call | solution.py:255
  123.8 8.3 %project_parts.3 = (bf16[1536,768]{1,0:T(8,128)(2,1)}, bf16[1536,768]{1,0:T(8,128)(2,1)}) custom-call(s32[5]{0:T(128)} %stack.221.where_ref, bf16[4,96,768]{2,1,0:T(8,128)(2,1)} %copy-done.12, bf16[4,96,768]{2,1,0:T(8,128)(2,1)} %copy-done.34, bf16[4,96,768]{2,1,0:T(8,128)(2,1)} %copy-done.35, bf16[4,96,768]{2,1,0:T(8,128)(2,1)} %copy-done.36, ...), custom_call_target="tpu_custom_call" | custom-call | flops 1 | bytes 1 | tf_op jit(solution)/shard_map/project_parts/pallas_call | solution.py:81
  132.1 11.0 %attend.3 = (bf16[384,384]{1,0:T(8,128)(2,1)}, f32[3,8,384]{2,1,0:T(8,128)}) custom-call(s32[3]{0:T(128)} %add_add_fusion.1.scalars_ref, bf16[768,1152]{1,0:T(8,128)(2,1)} %get-tuple-element.69.q_ref.kn_ref.vn_ref, bf16[768,1152]{1,0:T(8,128)(2,1)} %get-tuple-element.69.q_ref.kn_ref.vn_ref, bf16[768,1152]{1,0:T(8,128)(2,1)} %get-tuple-element.69.q_ref.kn_ref.vn_ref, ...), custom_call_target="tpu_custom_call" | custom-call | flops 1 | bytes 1 | tf_op jit(solution)/shard_map/attend/pallas_call | solution.py:255
  150.1 23.3 %feed_forward.1 = (bf16[384,768]{1,0:T(8,128)(2,1)}, f32[384,768]{1,0:T(8,128)}, bf16[384,768]{1,0:T(8,128)(2,1)}, bf16[768,6272]{1,0:T(8,128)(2,1)}, bf16[384,7...) custom-call(s32[1]{0:T(128)} %bitcast.core_ref, bf16[384,768]{1,0:T(8,128)(2,1)} %bitcast.293, bf16[384,768]{1,0:T(8,128)(2,1)} %bitcast.263, ...), custom_call_target="tpu_custom_call" | custom-call | flops 1 | bytes 1 | tf_op jit(solution)/shard_map/feed_forward/pallas_call | solution.py:545
  179.1 19.0 %attend_back.2 = (bf16[1536,768]{1,0:T(8,128)(2,1)}, bf16[384,1152]{1,0:T(8,128)(2,1)}, f32[8,1152]{1,0:T(8,128)}) custom-call(s32[3]{0:T(128)} %add_add_fusion.scalars_ref, bf16[768,1152]{1,0:T(8,128)(2,1)} %get-tuple-element.69.q_ref.kn_ref.vn_ref, bf16[768,1152]{1,0:T(8,128)(2,1)} %get-tuple-element.69.q_ref.kn_ref.vn_ref, ...), custom_call_target="tpu_custom_call" | custom-call | flops 1 | bytes 1 | tf_op jit(solution)/shard_map/attend_back/pallas_call | solution.py:370
  198.0 2.3 convolution_convert_fusion.3
  217.6 18.6 %attend_back.3 = (bf16[1536,768]{1,0:T(8,128)(2,1)}, bf16[384,1152]{1,0:T(8,128)(2,1)}, f32[8,1152]{1,0:T(8,128)}) custom-call(s32[3]{0:T(128)} %add_add_fusion.1.scalars_ref, bf16[768,1152]{1,0:T(8,128)(2,1)} %get-tuple-element.69.q_ref.kn_ref.vn_ref, bf16[768,1152]{1,0:T(8,128)(2,1)} %get-tuple-element.69.q_ref.kn_ref.vn_ref, ...), custom_call_target="tpu_custom_call" | custom-call | flops 1 | bytes 1 | tf_op jit(solution)/shard_map/attend_back/pallas_call | solution.py:370
  238.1 2.4 convolution_convert_fusion.2
  249.7 2.1 convolution_add_fusion.1
  267.7 9.1 %collective-permute-done.33 = bf16[4,104,768]{2,1,0:T(8,128)(2,1)S(1)} collective-permute-done((bf16[4,104,768]{2,1,0:T(8,128)(2,1)S(1)}, bf16[4,104,768]{2,1,0:T(8,128)(2,1)S(1)}, u32[]{:S(2)}, u32[]{:S(2)}) %collective-permute-start.33) | collective-permute-done | bytes 639008 | tf_op jit(solution)/shard_map/ppermute | solution.py:589
  279.0 2.2 collective-permute-start.36
  283.1 3.4 collective-permute-done.34
  286.5 6.9 %collective-permute-done.36 = bf16[104,768]{1,0:T(8,128)(2,1)S(1)} collective-permute-done((bf16[104,768]{1,0:T(8,128)(2,1)S(1)}, bf16[104,768]{1,0:T(8,128)(2,1)S(1)}, u32[]{:S(2)}, u32[]{:S(2)}) %collective-permute-start.36) | collective-permute-done | bytes 159776 | tf_op jit(solution)/shard_map/ppermute | solution.py:596
  293.4 11.0 %collective-permute-done.35 = bf16[104,768]{1,0:T(8,128)(2,1)S(1)} collective-permute-done((bf16[104,768]{1,0:T(8,128)(2,1)S(1)}, bf16[104,768]{1,0:T(8,128)(2,1)S(1)}, u32[]{:S(2)}, u32[]{:S(2)}) %collective-permute-start.35) | collective-permute-done | bytes 159776 | tf_op jit(solution)/shard_map/ppermute | solution.py:596
  310.6 2.5 fusion.14
  313.2 16.7 %reduce-scatter.4.cloned.1.call-done = bf16[24,6272]{1,0:T(8,128)(2,1)} async-done(((bf16[768,6272]{1,0:T(8,128)(2,1)}), bf16[24,6272]{1,0:T(8,128)(2,1)}) %reduce-scatter.4.cloned.1.call-update) | async-done | bytes 301072
  339.1 2.6 reshape.332
  341.7 2.3 collective-permute-done.38
  345.4 3.6 collective-permute-start.41
  352.0 4.6 %collective-permute-done.40 = bf16[48,1152]{1,0:T(8,128)(2,1)S(1)} collective-permute-done((bf16[48,1152]{1,0:T(8,128)(2,1)S(1)}, bf16[48,1152]{1,0:T(8,128)(2,1)S(1)}, u32[]{:S(2)}, u32[]{:S(2)}) %collective-permute-start.40) | collective-permute-done | bytes 110624 | tf_op jit(solution)/shard_map/ppermute | solution.py:596
  (384 shorter events, 128.5 us)
Async XLA Ops:
  7.3 141.1 %all-gather.2.cloned.1.call-start = ((), (), s32[]{:S(2)}) async-start(), calls=%async_computation.1 | async-start | bytes 11151360 | tf_op jit(solution)/shard_map/all_gather | solution.py:732
  9.9 27.0 %collective-permute-start = (bf16[2,2,96,768]{3,2,1,0:T(8,128)(2,1)}, bf16[2,2,96,768]{3,2,1,0:T(8,128)(2,1)S(1)}, u32[]{:S(2)}, u32[]{:S(2)}) collective-permute-start(bf16[2,2,96,768]{3,2,1,0:T(8,128)(2,1)} %param.16), channel_id=1, source_target_pairs={{0,1},{1,0},{2,3},{3,2},{4,5},{5,4},{6,7},{7,6},{8,9},{9,8},{10,11... | collective-permute-start | bytes 1769480 | tf_op jit(solution)/shard_map/ppermute | solution.py:586
  21.3 10.8 %collective-permute-start.4 = (bf16[48,1152]{1,0:T(8,128)(2,1)}, bf16[48,1152]{1,0:T(8,128)(2,1)S(1)}, u32[]{:S(2)}, u32[]{:S(2)}) collective-permute-start(bf16[48,1152]{1,0:T(8,128)(2,1)} %bitcast.141), channel_id=1, source_target_pairs={{0,8},{1,9},{2,10},{3,11},{4,12},{5,13},{6,14},{7,15},{8,0},{9,1},... | collective-permute-start | bytes 331784 | tf_op jit(solution)/shard_map/ppermute | solution.py:596
  21.3 10.8 %collective-permute-start.3 = (bf16[48,1152]{1,0:T(8,128)(2,1)}, bf16[48,1152]{1,0:T(8,128)(2,1)S(1)}, u32[]{:S(2)}, u32[]{:S(2)}) collective-permute-start(bf16[48,1152]{1,0:T(8,128)(2,1)} %bitcast.141), channel_id=1, source_target_pairs={{0,4},{1,5},{2,6},{3,7},{4,8},{5,9},{6,10},{7,11},{8,12},{9,13},{1... | collective-permute-start | bytes 331784 | tf_op jit(solution)/shard_map/ppermute | solution.py:596
  33.9 12.0 %collective-permute-start.10 = (bf16[4,48,1152]{2,1,0:T(8,128)(2,1)S(1)}, bf16[4,48,1152]{2,1,0:T(8,128)(2,1)}, u32[]{:S(2)}, u32[]{:S(2)}) collective-permute-start(bf16[4,48,1152]{2,1,0:T(8,128)(2,1)S(1)} %pad_maximum_fusion.7.refs_0_), channel_id=1, source_target_pairs={{0,16},{16,0},{1,17},{17,1},{2,18},{18,2},{3,19},{19,3},{4,20},{20... | collective-permute-start | bytes 1327112 | tf_op jit(solution)/shard_map/ppermute | solution.py:592
  35.5 11.6 %collective-permute-start.9 = (bf16[4,48,1152]{2,1,0:T(8,128)(2,1)S(1)}, bf16[4,48,1152]{2,1,0:T(8,128)(2,1)}, u32[]{:S(2)}, u32[]{:S(2)}) collective-permute-start(bf16[4,48,1152]{2,1,0:T(8,128)(2,1)S(1)} %pad_maximum_fusion.7.refs_0_), channel_id=1, source_target_pairs={{0,2},{1,3},{2,0},{3,1},{4,6},{5,7},{6,4},{7,5},{8,10},{9,11},{10,... | collective-permute-start | bytes 1327112 | tf_op jit(solution)/shard_map/ppermute | solution.py:589
  37.0 10.1 %collective-permute-start.8 = (bf16[104,768]{1,0:T(8,128)(2,1)S(1)}, bf16[104,768]{1,0:T(8,128)(2,1)}, u32[]{:S(2)}, u32[]{:S(2)}) collective-permute-start(bf16[104,768]{1,0:T(8,128)(2,1)S(1)} %fusion.56), channel_id=1, source_target_pairs={{0,12},{1,13},{2,14},{3,15},{4,0},{5,1},{6,2},{7,3},{8,4},{9,5},{1... | collective-permute-start | bytes 479240 | tf_op jit(solution)/shard_map/ppermute | solution.py:596
  38.4 14.1 %collective-permute-start.7 = (bf16[104,768]{1,0:T(8,128)(2,1)S(1)}, bf16[104,768]{1,0:T(8,128)(2,1)}, u32[]{:S(2)}, u32[]{:S(2)}) collective-permute-start(bf16[104,768]{1,0:T(8,128)(2,1)S(1)} %fusion.56), channel_id=1, source_target_pairs={{0,8},{1,9},{2,10},{3,11},{4,12},{5,13},{6,14},{7,15},{8,0},{9,1},... | collective-permute-start | bytes 479240 | tf_op jit(solution)/shard_map/ppermute | solution.py:596
  39.1 13.4 %collective-permute-start.6 = (bf16[104,768]{1,0:T(8,128)(2,1)S(1)}, bf16[104,768]{1,0:T(8,128)(2,1)}, u32[]{:S(2)}, u32[]{:S(2)}) collective-permute-start(bf16[104,768]{1,0:T(8,128)(2,1)S(1)} %fusion.56), channel_id=1, source_target_pairs={{0,4},{1,5},{2,6},{3,7},{4,8},{5,9},{6,10},{7,11},{8,12},{9,13},{1... | collective-permute-start | bytes 479240 | tf_op jit(solution)/shard_map/ppermute | solution.py:596
  52.5 277.4 %reduce-scatter.4.cloned.1.call-start = ((), (), s32[]{:S(2)}) async-start(), calls=%async_computation.2 | async-start | bytes 9934848
  53.8 16.7 %collective-permute-start.11 = (bf16[4,104,768]{2,1,0:T(8,128)(2,1)S(1)}, bf16[4,104,768]{2,1,0:T(8,128)(2,1)}, u32[]{:S(2)}, u32[]{:S(2)}) collective-permute-start(bf16[4,104,768]{2,1,0:T(8,128)(2,1)S(1)} %pad_maximum_fusion.4.a_ref), channel_id=1, source_target_pairs={{0,2},{1,3},{2,0},{3,1},{4,6},{5,7},{6,4},{7,5},{8,10},{9,11},{10,... | collective-permute-start | bytes 1916936 | tf_op jit(solution)/shard_map/ppermute | solution.py:589
  55.0 16.4 %collective-permute-start.14 = (bf16[96,768]{1,0:T(8,128)(2,1)S(1)}, bf16[96,768]{1,0:T(8,128)(2,1)S(1)}, u32[]{:S(2)}, u32[]{:S(2)}) collective-permute-start(bf16[96,768]{1,0:T(8,128)(2,1)S(1)} %get-tuple-element.66), channel_id=1, source_target_pairs={{0,12},{1,13},{2,14},{3,15},{4,0},{5,1},{6,2},{7,3},{8,4},{9,5},{1... | collective-permute-start | bytes 442376 | tf_op jit(solution)/shard_map/ppermute | solution.py:596
  55.1 21.1 %collective-permute-start.13 = (bf16[96,768]{1,0:T(8,128)(2,1)S(1)}, bf16[96,768]{1,0:T(8,128)(2,1)S(1)}, u32[]{:S(2)}, u32[]{:S(2)}) collective-permute-start(bf16[96,768]{1,0:T(8,128)(2,1)S(1)} %get-tuple-element.66), channel_id=1, source_target_pairs={{0,8},{1,9},{2,10},{3,11},{4,12},{5,13},{6,14},{7,15},{8,0},{9,1},... | collective-permute-start | bytes 442376 | tf_op jit(solution)/shard_map/ppermute | solution.py:596
  56.4 19.8 %collective-permute-start.12 = (bf16[96,768]{1,0:T(8,128)(2,1)S(1)}, bf16[96,768]{1,0:T(8,128)(2,1)S(1)}, u32[]{:S(2)}, u32[]{:S(2)}) collective-permute-start(bf16[96,768]{1,0:T(8,128)(2,1)S(1)} %get-tuple-element.66), channel_id=1, source_target_pairs={{0,4},{1,5},{2,6},{3,7},{4,8},{5,9},{6,10},{7,11},{8,12},{9,13},{1... | collective-permute-start | bytes 442376 | tf_op jit(solution)/shard_map/ppermute | solution.py:596
  58.6 19.1 %collective-permute-start.16 = (bf16[4,48,1152]{2,1,0:T(8,128)(2,1)}, bf16[4,48,1152]{2,1,0:T(8,128)(2,1)S(1)}, u32[]{:S(2)}, u32[]{:S(2)}) collective-permute-start(bf16[4,48,1152]{2,1,0:T(8,128)(2,1)} %collective-permute-done.9.refs_1_), channel_id=1, source_target_pairs={{0,16},{16,0},{1,17},{17,1},{2,18},{18,2},{3,19},{19,3},{4,20},{20... | collective-permute-start | bytes 1327112 | tf_op jit(solution)/shard_map/ppermute | solution.py:592
  77.7 16.1 %collective-permute-start.17 = (bf16[4,104,768]{2,1,0:T(8,128)(2,1)S(1)}, bf16[4,104,768]{2,1,0:T(8,128)(2,1)S(1)}, u32[]{:S(2)}, u32[]{:S(2)}) collective-permute-start(bf16[4,104,768]{2,1,0:T(8,128)(2,1)S(1)} %pad_maximum_fusion.4.a_ref), channel_id=1, source_target_pairs={{0,1},{1,0},{2,3},{3,2},{4,5},{5,4},{6,7},{7,6},{8,9},{9,8},{10,11... | collective-permute-start | bytes 1916936 | tf_op jit(solution)/shard_map/ppermute | solution.py:586
  91.5 15.3 %collective-permute-start.19 = (bf16[4,96,768]{2,1,0:T(8,128)(2,1)S(1)}, bf16[4,96,768]{2,1,0:T(8,128)(2,1)S(1)}, u32[]{:S(2)}, u32[]{:S(2)}) collective-permute-start(bf16[4,96,768]{2,1,0:T(8,128)(2,1)S(1)} %pad_maximum_fusion.5.a_ref), channel_id=1, source_target_pairs={{0,2},{1,3},{2,0},{3,1},{4,6},{5,7},{6,4},{7,5},{8,10},{9,11},{10,... | collective-permute-start | bytes 1769480 | tf_op jit(solution)/shard_map/ppermute | solution.py:589
  93.8 28.4 %collective-permute-start.20 = (bf16[4,96,768]{2,1,0:T(8,128)(2,1)S(1)}, bf16[4,96,768]{2,1,0:T(8,128)(2,1)S(1)}, u32[]{:S(2)}, u32[]{:S(2)}) collective-permute-start(bf16[4,96,768]{2,1,0:T(8,128)(2,1)S(1)} %pad_maximum_fusion.5.a_ref), channel_id=1, source_target_pairs={{0,1},{1,0},{2,3},{3,2},{4,5},{5,4},{6,7},{7,6},{8,9},{9,8},{10,11... | collective-permute-start | bytes 1769480 | tf_op jit(solution)/shard_map/ppermute | solution.py:586
  106.9 15.4 %collective-permute-start.21 = (bf16[4,96,768]{2,1,0:T(8,128)(2,1)S(1)}, bf16[4,96,768]{2,1,0:T(8,128)(2,1)S(1)}, u32[]{:S(2)}, u32[]{:S(2)}) collective-permute-start(bf16[4,96,768]{2,1,0:T(8,128)(2,1)S(1)} %collective-permute-done.19.b_ref), channel_id=1, source_target_pairs={{0,1},{1,0},{2,3},{3,2},{4,5},{5,4},{6,7},{7,6},{8,9},{9,8},{10,11... | collective-permute-start | bytes 1769480 | tf_op jit(solution)/shard_map/ppermute | solution.py:586
  210.5 25.7 %collective-permute-start.26 = (bf16[4,2,24,768]{3,2,0,1:T(8,128)(2,1)S(1)}, bf16[4,2,24,768]{3,2,0,1:T(8,128)(2,1)S(1)}, u32[]{:S(2)}, u32[]{:S(2)}) collective-permute-start(bf16[4,2,24,768]{3,2,0,1:T(8,128)(2,1)S(1)} %bitcast.310), channel_id=1, source_target_pairs={{0,16},{16,0},{1,17},{17,1},{2,18},{18,2},{3,19},{19,3},{4,20},{20... | collective-permute-start | bytes 884744 | tf_op jit(solution)/shard_map/ppermute | solution.py:592
  216.0 46.2 %collective-permute-start.27 = (bf16[4,96,768]{2,1,0:T(8,128)(2,1)}, bf16[4,96,768]{2,1,0:T(8,128)(2,1)}, u32[]{:S(2)}, u32[]{:S(2)}) collective-permute-start(bf16[4,96,768]{2,1,0:T(8,128)(2,1)} %dynamic-slice_bitcast_fusion.2), channel_id=1, source_target_pairs={{0,2},{1,3},{2,0},{3,1},{4,6},{5,7},{6,4},{7,5},{8,10},{9,11},{10,... | collective-permute-start | bytes 1769480 | tf_op jit(solution)/shard_map/ppermute | solution.py:589
  237.6 23.6 %collective-permute-start.28 = (bf16[4,24,768]{2,1,0:T(8,128)(2,1)}, bf16[4,24,768]{2,1,0:T(8,128)(2,1)}, u32[]{:S(2)}, u32[]{:S(2)}) collective-permute-start(bf16[4,24,768]{2,1,0:T(8,128)(2,1)} %dynamic-slice_bitcast_fusion.9), channel_id=1, source_target_pairs={{0,2},{1,3},{2,0},{3,1},{4,6},{5,7},{6,4},{7,5},{8,10},{9,11},{10,... | collective-permute-start | bytes 442376 | tf_op jit(solution)/shard_map/ppermute | solution.py:589
  244.5 13.3 %collective-permute-start.32 = (bf16[10,96,768]{2,1,0:T(8,128)(2,1)}, bf16[10,96,768]{2,1,0:T(8,128)(2,1)}, u32[]{:S(2)}, u32[]{:S(2)}) collective-permute-start(bf16[10,96,768]{2,1,0:T(8,128)(2,1)} %pad_maximum_fusion.1), channel_id=1, source_target_pairs={{0,1},{1,0},{2,3},{3,2},{4,5},{5,4},{6,7},{7,6},{8,9},{9,8},{10,11... | collective-permute-start | bytes 4423688 | tf_op jit(solution)/shard_map/ppermute | solution.py:586
  254.2 75.7 %collective-permute-start.37 = (bf16[4,2,48,1152]{3,2,0,1:T(8,128)(2,1)}, bf16[4,2,48,1152]{3,2,0,1:T(8,128)(2,1)}, u32[]{:S(2)}, u32[]{:S(2)}) collective-permute-start(bf16[4,2,48,1152]{3,2,0,1:T(8,128)(2,1)} %copy_bitcast_fusion), channel_id=1, source_target_pairs={{0,16},{16,0},{1,17},{17,1},{2,18},{18,2},{3,19},{19,3},{4,20},{20... | collective-permute-start | bytes 2654216 | tf_op jit(solution)/shard_map/ppermute | solution.py:592
  259.8 17.0 %collective-permute-start.33 = (bf16[4,104,768]{2,1,0:T(8,128)(2,1)S(1)}, bf16[4,104,768]{2,1,0:T(8,128)(2,1)S(1)}, u32[]{:S(2)}, u32[]{:S(2)}) collective-permute-start(bf16[4,104,768]{2,1,0:T(8,128)(2,1)S(1)} %fusion.23), channel_id=1, source_target_pairs={{0,2},{1,3},{2,0},{3,1},{4,6},{5,7},{6,4},{7,5},{8,10},{9,11},{10,... | collective-permute-start | bytes 1916936 | tf_op jit(solution)/shard_map/ppermute | solution.py:589
  263.5 15.5 %collective-permute-start.31 = (bf16[120,768]{1,0:T(8,128)(2,1)S(1)}, bf16[120,768]{1,0:T(8,128)(2,1)S(1)}, u32[]{:S(2)}, u32[]{:S(2)}) collective-permute-start(bf16[120,768]{1,0:T(8,128)(2,1)S(1)} %get-tuple-element.123), channel_id=1, source_target_pairs={{0,12},{1,13},{2,14},{3,15},{4,0},{5,1},{6,2},{7,3},{8,4},{9,5},{1... | collective-permute-start | bytes 552968 | tf_op jit(solution)/shard_map/ppermute | solution.py:596
  263.6 17.6 %collective-permute-start.29 = (bf16[120,768]{1,0:T(8,128)(2,1)S(1)}, bf16[120,768]{1,0:T(8,128)(2,1)S(1)}, u32[]{:S(2)}, u32[]{:S(2)}) collective-permute-start(bf16[120,768]{1,0:T(8,128)(2,1)S(1)} %get-tuple-element.124), channel_id=1, source_target_pairs={{0,4},{1,5},{2,6},{3,7},{4,8},{5,9},{6,10},{7,11},{8,12},{9,13},{1... | collective-permute-start | bytes 552968 | tf_op jit(solution)/shard_map/ppermute | solution.py:596
  265.6 15.6 %collective-permute-start.30 = (bf16[120,768]{1,0:T(8,128)(2,1)S(1)}, bf16[120,768]{1,0:T(8,128)(2,1)S(1)}, u32[]{:S(2)}, u32[]{:S(2)}) collective-permute-start(bf16[120,768]{1,0:T(8,128)(2,1)S(1)} %get-tuple-element.125), channel_id=1, source_target_pairs={{0,8},{1,9},{2,10},{3,11},{4,12},{5,13},{6,14},{7,15},{8,0},{9,1},... | collective-permute-start | bytes 552968 | tf_op jit(solution)/shard_map/ppermute | solution.py:596
  277.1 9.4 %collective-permute-start.34 = (bf16[104,768]{1,0:T(8,128)(2,1)S(1)}, bf16[104,768]{1,0:T(8,128)(2,1)S(1)}, u32[]{:S(2)}, u32[]{:S(2)}) collective-permute-start(bf16[104,768]{1,0:T(8,128)(2,1)S(1)} %get-tuple-element.126), channel_id=1, source_target_pairs={{0,4},{1,5},{2,6},{3,7},{4,8},{5,9},{6,10},{7,11},{8,12},{9,13},{1... | collective-permute-start | bytes 479240 | tf_op jit(solution)/shard_map/ppermute | solution.py:596
  279.0 14.4 %collective-permute-start.36 = (bf16[104,768]{1,0:T(8,128)(2,1)S(1)}, bf16[104,768]{1,0:T(8,128)(2,1)S(1)}, u32[]{:S(2)}, u32[]{:S(2)}) collective-permute-start(bf16[104,768]{1,0:T(8,128)(2,1)S(1)} %get-tuple-element.127), channel_id=1, source_target_pairs={{0,12},{1,13},{2,14},{3,15},{4,0},{5,1},{6,2},{7,3},{8,4},{9,5},{1... | collective-permute-start | bytes 479240 | tf_op jit(solution)/shard_map/ppermute | solution.py:596
  281.2 23.3 %collective-permute-start.35 = (bf16[104,768]{1,0:T(8,128)(2,1)S(1)}, bf16[104,768]{1,0:T(8,128)(2,1)S(1)}, u32[]{:S(2)}, u32[]{:S(2)}) collective-permute-start(bf16[104,768]{1,0:T(8,128)(2,1)S(1)} %get-tuple-element.128), channel_id=1, source_target_pairs={{0,8},{1,9},{2,10},{3,11},{4,12},{5,13},{6,14},{7,15},{8,0},{9,1},... | collective-permute-start | bytes 479240 | tf_op jit(solution)/shard_map/ppermute | solution.py:596
  333.1 10.9 %collective-permute-start.38 = (bf16[4,48,1152]{2,1,0:T(8,128)(2,1)}, bf16[4,48,1152]{2,1,0:T(8,128)(2,1)}, u32[]{:S(2)}, u32[]{:S(2)}) collective-permute-start(bf16[4,48,1152]{2,1,0:T(8,128)(2,1)} %dynamic-slice_bitcast_fusion.3), channel_id=1, source_target_pairs={{0,2},{1,3},{2,0},{3,1},{4,6},{5,7},{6,4},{7,5},{8,10},{9,11},{10,... | collective-permute-start | bytes 1327112 | tf_op jit(solution)/shard_map/ppermute | solution.py:589
  (82 other events, 484.9 us)
Sparse Core Ops, SparseCore 0:
  52.6 91.6 all-gather.1
  177.1 152.8 reduce-scatter.3
where the time goes:
time: 375 us; the launch traced here: 367 us
  Pallas kernels  108 us (29%)
  waiting for transfers between devices  93.6 us (25%)
  local copies, waits for them, and re-layouts  51.9 us (14%)
  other arithmetic  42.3 us (11%)
  starting transfers between devices  40 us (11%)
  between operations  16 us (4%)
  matrix products  15.6 us (4%)
    ppermute x18, waiting for transfers between devices, along_z(): lax.ppermute(array, 'ctx', [(i, (i + 4 * hop) % count) for i in range(cou...  43.8 us
    pallas_call x2, Pallas kernels, attend_back(): pl.pallas_call(functools.partial(attend_back_kernel, block=block), grid_s...  37.5 us
    ppermute x7, waiting for transfers between devices, over_y(): return lax.ppermute(array, 'ctx', [(i, i ^ 2) for i in range(self.count)])  25.8 us
    ppermute x18, starting transfers between devices, along_z(): lax.ppermute(array, 'ctx', [(i, (i + 4 * hop) % count) for i in range(cou...  23.7 us
    pallas_call x1, Pallas kernels, feed_forward(): pl.pallas_call(functools.partial(feed_forward_kernel, pairs=pairs, joined...  23.3 us
    pallas_call x2, Pallas kernels, attend(): pl.pallas_call(functools.partial(attend_kernel, block=block), grid_spec=s...  21.8 us
    unnamed x3, waiting for transfers between devices  16.7 us
    pallas_call x2, Pallas kernels, project_parts(): pl.pallas_call(functools.partial(project_parts_kernel, start=start, turne...  16.7 us
  transfers between devices with their start and end apart: 47, of which 20 were waited for; matrix products, arithmetic and copies ran while one was open for 23% of the time, Pallas kernels for 23%

commit v1 on v0

--- a/solution.py
+++ b/solution.py
@@ -382,9 +382,9 @@
 
 
 def feed_forward_kernel(
-    core_ref, attn_ref, x_ref, top_ref, up_ref, down_ref, out_ref, vec_ref,
-    block_out_ref, hidden_grad_ref, attn_grad_ref, weights_ref, mine_ref, theirs_ref,
-    hidden, unit, inverse, normed, normed_flipped, lowered, grad_normed,
+    core_ref, attn_ref, x_ref, top_ref, up_ref, down_ref, out_ref, tile_ref,
+    block_out_ref, hidden_grad_ref, own_grad_ref, far_grad_ref, weights_ref, mine_ref, theirs_ref,
+    vec_ref, hidden, unit, inverse, normed, normed_flipped, lowered, grad_normed,
     up_grads, join_grads, down_grads, out_grads, vec_grads, sums, up_sems, join_sems, down_sems, last_sems,
     *, pairs, joined
 ):
@@ -394,6 +394,7 @@
 
     @pl.when(chunk == 0)
     def _():
+        vec_ref[...] = tile_ref[...].astype(F32).T
         value = (
             x_ref[...].astype(F32)
             + jnp.dot(attn_ref[...], out_ref[...], preferred_element_type=F32)
@@ -481,7 +482,15 @@
         hidden_grad_ref[...] = grad
         sums[0:1, :] = jnp.sum(grad, 0, keepdims=True)
         low = grad.astype(BF16)
-        attn_grad_ref[...] = nt_dot(low, out_ref[...]).astype(BF16)
+        attn_grad = nt_dot(low, out_ref[...]).astype(BF16)
+        for core in range(2):
+            own, far = core * (width // 2), (1 - core) * (width // 2)
+
+            @pl.when(core_ref[0] == core)
+            def _():
+                own_grad_ref[...] = attn_grad[:, own : own + width // 2]
+                far_grad_ref[...] = attn_grad[:, far : far + width // 2]
+
         out_grads[...] = jnp.dot(
             attn_ref[...].astype(F32).T.astype(BF16), low, preferred_element_type=F32
         ).astype(BF16)
@@ -504,11 +513,12 @@
             copy.wait()
 
 
-def feed_forward(core, attn, x, top, weights, vectors, chunks, pairs, joined):
+def feed_forward(core, attn, x, top, weights, chunks, pairs, joined):
     rows, width = x.shape
     apart = chunks - joined
     fixed = lambda b, c: (0, 0)
     whole = pl.BlockSpec((rows, width), fixed)
+    halved = pl.BlockSpec((rows, width // 2), fixed)
     spec = pltpu.PrefetchScalarGridSpec(
         num_scalar_prefetch=1,
         grid=(chunks,),
@@ -519,10 +529,11 @@
             pl.BlockSpec((width, width), lambda b, c: (0, b)),
             pl.BlockSpec((width, width), lambda b, c: (0, chunks + b)),
             pl.BlockSpec((width, width), lambda b, c: (0, 2 * chunks)),
-            pl.BlockSpec(vectors.shape, fixed),
-        ],
-        out_specs=[whole, whole, whole] + [pl.BlockSpec(memory_space=pl.ANY)] * 3,
+            pl.BlockSpec((width, LANES), lambda b, c: (0, weights.shape[1] // LANES - 1)),
+        ],
+        out_specs=[whole, whole, halved, halved] + [pl.BlockSpec(memory_space=pl.ANY)] * 3,
         scratch_shapes=[
+            pltpu.VMEM((LANES, width), F32),
             pltpu.VMEM((rows, width), F32),
             pltpu.VMEM((rows, width), F32),
             pltpu.VMEM((rows, 1), F32),
@@ -548,7 +559,8 @@
         out_shape=[
             jax.ShapeDtypeStruct((rows, width), BF16),
             jax.ShapeDtypeStruct((rows, width), F32),
-            jax.ShapeDtypeStruct((rows, width), BF16),
+            jax.ShapeDtypeStruct((rows, width // 2), BF16),
+            jax.ShapeDtypeStruct((rows, width // 2), BF16),
             jax.ShapeDtypeStruct((width, weights.shape[1] - apart * width), BF16),
             jax.ShapeDtypeStruct((width // 2, apart * width), BF16),
             jax.ShapeDtypeStruct((width // 2, apart * width), BF16),
@@ -556,7 +568,7 @@
         compiler_params=pltpu.CompilerParams(vmem_limit_bytes=VMEM_LIMIT),
         cost_estimate=LIGHT,
         name="feed_forward",
-    )(core.reshape(1), attn, x, top, weights, weights, weights, vectors)
+    )(core.reshape(1), attn, x, top, weights, weights, weights, weights)
 
 
 def after(value, *others):
@@ -730,7 +742,6 @@
     vec_piece = jnp.pad(vec_piece, ((0, 0), (0, LANES - vec_piece.shape[1])))
     packed = after(jnp.concatenate([up_piece, down_piece, out_weight, vec_piece], 1), *weights_gate)
     weights = lax.all_gather(packed, ("batch", "ctx"), axis=0, tiled=True)
-    vectors = weights[:, -LANES:].T[: 4 + folds].astype(F32)
 
     inputs_pair = ordered(core, layer_input, inputs_got, 2).reshape(seqs, rows, width)
 
@@ -760,8 +771,8 @@
     flat_inputs = layer_input.reshape(-1, width)
     joined = folds * 3 // 4
     apart = folds - joined
-    output, grad_hidden, grad_attn, weight_grads, down_mine, down_theirs = feed_forward(
-        core, attn_low, flat_inputs, cotangent.reshape(-1, width), weights, vectors, folds, links.count, joined
+    output, grad_hidden, grad_mine, grad_theirs, weight_grads, down_mine, down_theirs = feed_forward(
+        core, attn_low, flat_inputs, cotangent.reshape(-1, width), weights, folds, links.count, joined
     )
     output = output.reshape(layer_input.shape)
     packed = lax.psum_scatter(weight_grads, ("batch", "ctx"), scatter_dimension=0, tiled=True)
@@ -771,11 +782,10 @@
     down_sent = pick(down_part, 1 - links.x)
     down_got = links.over_x(down_sent)
 
-    grad_split = grad_attn.reshape(-1, 2, half)
-    grad_got = links.over_core(pick(grad_split, 1 - core, 1))
+    grad_got = links.over_core(grad_theirs)
     grad_rows = ordered(
         core,
-        pick(grad_split, core, 1).reshape(seqs, 2, pos_dev, half),
+        grad_mine.reshape(seqs, 2, pos_dev, half),
         grad_got.reshape(seqs, 2, pos_dev, half),
         2,
     ).reshape(seqs, rows, half)

time: 375 us -> 371 us (0.989)
  local copies, waits for them, and re-layouts: 51.9 us -> 46.4 us
where the time goes in v1:
time: 371 us; the launch traced here: 364 us
  Pallas kernels  108 us (29%)
  waiting for transfers between devices  96.5 us (26%)
  local copies, waits for them, and re-layouts  46.4 us (13%)
  other arithmetic  41.3 us (11%)
  starting transfers between devices  40.1 us (11%)
  between operations  15.7 us (4%)
  matrix products  15.6 us (4%)
    ppermute x18, waiting for transfers between devices, along_z(): lax.ppermute(array, 'ctx', [(i, (i + 4 * hop) % count) for i in range(cou...  43.2 us
    pallas_call x2, Pallas kernels, attend_back(): pl.pallas_call(functools.partial(attend_back_kernel, block=block), grid_s...  37.7 us
    ppermute x7, waiting for transfers between devices, over_y(): return lax.ppermute(array, 'ctx', [(i, i ^ 2) for i in range(self.count)])  26 us
    pallas_call x1, Pallas kernels, feed_forward(): pl.pallas_call(functools.partial(feed_forward_kernel, pairs=pairs, joined...  23.6 us
    ppermute x18, starting transfers between devices, along_z(): lax.ppermute(array, 'ctx', [(i, (i + 4 * hop) % count) for i in range(cou...  23.3 us
    pallas_call x2, Pallas kernels, attend(): pl.pallas_call(functools.partial(attend_kernel, block=block), grid_spec=s...  21.8 us
    unnamed x3, waiting for transfers between devices  17.4 us
    pallas_call x2, Pallas kernels, project_parts(): pl.pallas_call(functools.partial(project_parts_kernel, start=start, turne...  16.7 us
  transfers between devices with their start and end apart: 47, of which 20 were waited for; matrix products, arithmetic and copies ran while one was open for 23% of the time, Pallas kernels for 23%

profile of v1, /device:TPU:0, one launch (start us, length us, event | category | flops | bytes accessed | tf_op | source)
XLA Modules:
  0.0 364.0 jit_solution(14232749264810350422)
XLA Ops:
  16.7 4.7 %collective-permute-start.5 = (bf16[48,1152]{1,0:T(8,128)(2,1)}, bf16[48,1152]{1,0:T(8,128)(2,1)S(1)}, u32[]{:S(2)}, u32[]{:S(2)}) collective-permute-start(bf16[48,1152]{1,0:T(8,128)(2,1)} %bitcast.143), channel_id=1, source_target_pairs={{0,12},{1,13},{2,14},{3,15},{4,0},{5,1},{6,2},{7,3},{8,4},{9,5},{1... | collective-permute-start | bytes 331784 | tf_op jit(solution)/shard_map/ppermute | solution.py:608
  22.4 2.8 fusion.20
  25.3 6.9 %collective-permute-done.4 = bf16[48,1152]{1,0:T(8,128)(2,1)S(1)} collective-permute-done((bf16[48,1152]{1,0:T(8,128)(2,1)}, bf16[48,1152]{1,0:T(8,128)(2,1)S(1)}, u32[]{:S(2)}, u32[]{:S(2)}) %collective-permute-start.4) | collective-permute-done | bytes 110624 | tf_op jit(solution)/shard_map/ppermute | solution.py:608
  42.6 3.3 collective-permute-done.10.refs_2_
  47.1 5.4 %collective-permute-done.7 = bf16[104,768]{1,0:T(8,128)(2,1)} collective-permute-done((bf16[104,768]{1,0:T(8,128)(2,1)S(1)}, bf16[104,768]{1,0:T(8,128)(2,1)}, u32[]{:S(2)}, u32[]{:S(2)}) %collective-permute-start.7) | collective-permute-done | bytes 159776 | tf_op jit(solution)/shard_map/ppermute | solution.py:608
  60.2 10.3 %collective-permute-done.11.b_ref = bf16[4,104,768]{2,1,0:T(8,128)(2,1)} collective-permute-done((bf16[4,104,768]{2,1,0:T(8,128)(2,1)S(1)}, bf16[4,104,768]{2,1,0:T(8,128)(2,1)}, u32[]{:S(2)}, u32[]{:S(2)}) %collective-permute-start.11) | collective-permute-done | bytes 639008 | tf_op jit(solution)/shard_map/ppermute | solution.py:601
  71.4 4.8 %collective-permute-done.13 = bf16[96,768]{1,0:T(8,128)(2,1)S(1)} collective-permute-done((bf16[96,768]{1,0:T(8,128)(2,1)S(1)}, bf16[96,768]{1,0:T(8,128)(2,1)S(1)}, u32[]{:S(2)}, u32[]{:S(2)}) %collective-permute-start.13) | collective-permute-done | bytes 147488 | tf_op jit(solution)/shard_map/ppermute | solution.py:608
  78.5 3.4 place.1.refs_2_
  85.7 5.2 %project.1 = (bf16[768,1152]{1,0:T(8,128)(2,1)}, bf16[768,768]{1,0:T(8,128)(2,1)}) custom-call(bf16[768,768]{1,0:T(8,128)(2,1)} %bitcast.273, f32[1,768]{1,0:T(1,128)} %reshape.300.refs_0_, f32[1,768]{1,0:T(1,128)} %reshape.301.refs_1_, bf16[768,1152]{1,0:T(8,128)(2,1)} %place.1.refs_2_, f32[1,1152]{1,0:T(1,128)} %bitcast.319, f32[384,128]{1,0:T(8,128)} %bitcast.280, ...), custom_call_target="tpu_custom_call" | custom-call | flops 1 | bytes 1 | tf_op jit(solution)/shard_map/project/pallas_call | solution.py:100
  95.5 8.4 %project_parts.2 = (bf16[1536,768]{1,0:T(8,128)(2,1)}, bf16[1536,768]{1,0:T(8,128)(2,1)}) custom-call(s32[5]{0:T(128)} %stack.221.where_ref, bf16[4,104,768]{2,1,0:T(8,128)(2,1)} %copy-done.11, bf16[4,104,768]{2,1,0:T(8,128)(2,1)} %collective-permute-done.11.b_ref, bf16[4,104,768]{2,1,0:T(8,128)(2,1)} %copy-done.32, bf16[4,104,768]{2,1,0:T(8,128)(2,1)} %copy-done.33, ...), custom_call_target="tpu_custom_call" | custom-call | flops 1 | bytes 1 | tf_op jit(solution)/shard_map/project_parts/pallas_call | solution.py:81
  103.8 3.0 collective-permute-done.19.b_ref
  111.4 10.8 %attend.2 = (bf16[384,384]{1,0:T(8,128)(2,1)}, f32[3,8,384]{2,1,0:T(8,128)}) custom-call(s32[3]{0:T(128)} %add_add_fusion.scalars_ref, bf16[768,1152]{1,0:T(8,128)(2,1)} %get-tuple-element.70.q_ref.kn_ref.vn_ref, bf16[768,1152]{1,0:T(8,128)(2,1)} %get-tuple-element.70.q_ref.kn_ref.vn_ref, bf16[768,1152]{1,0:T(8,128)(2,1)} %get-tuple-element.70.q_ref.kn_ref.vn_ref, ...), custom_call_target="tpu_custom_call" | custom-call | flops 1 | bytes 1 | tf_op jit(solution)/shard_map/attend/pallas_call | solution.py:255
  123.9 8.3 %project_parts.3 = (bf16[1536,768]{1,0:T(8,128)(2,1)}, bf16[1536,768]{1,0:T(8,128)(2,1)}) custom-call(s32[5]{0:T(128)} %stack.221.where_ref, bf16[4,96,768]{2,1,0:T(8,128)(2,1)} %copy-done.12, bf16[4,96,768]{2,1,0:T(8,128)(2,1)} %copy-done.34, bf16[4,96,768]{2,1,0:T(8,128)(2,1)} %copy-done.35, bf16[4,96,768]{2,1,0:T(8,128)(2,1)} %copy-done.36, ...), custom_call_target="tpu_custom_call" | custom-call | flops 1 | bytes 1 | tf_op jit(solution)/shard_map/project_parts/pallas_call | solution.py:81
  132.2 11.0 %attend.3 = (bf16[384,384]{1,0:T(8,128)(2,1)}, f32[3,8,384]{2,1,0:T(8,128)}) custom-call(s32[3]{0:T(128)} %add_add_fusion.1.scalars_ref, bf16[768,1152]{1,0:T(8,128)(2,1)} %get-tuple-element.70.q_ref.kn_ref.vn_ref, bf16[768,1152]{1,0:T(8,128)(2,1)} %get-tuple-element.70.q_ref.kn_ref.vn_ref, bf16[768,1152]{1,0:T(8,128)(2,1)} %get-tuple-element.70.q_ref.kn_ref.vn_ref, ...), custom_call_target="tpu_custom_call" | custom-call | flops 1 | bytes 1 | tf_op jit(solution)/shard_map/attend/pallas_call | solution.py:255
  148.4 23.6 %feed_forward.1 = (bf16[384,768]{1,0:T(8,128)(2,1)}, f32[384,768]{1,0:T(8,128)}, bf16[384,384]{1,0:T(8,128)(2,1)}, bf16[384,384]{1,0:T(8,128)(2,1)}, bf16[768,62...) custom-call(s32[1]{0:T(128)} %bitcast.core_ref, bf16[384,768]{1,0:T(8,128)(2,1)} %bitcast.293, ...), custom_call_target="tpu_custom_call" | custom-call | flops 1 | bytes 1 | tf_op jit(solution)/shard_map/feed_forward/pallas_call | solution.py:556
  174.8 19.2 %attend_back.2 = (bf16[1536,768]{1,0:T(8,128)(2,1)}, bf16[384,1152]{1,0:T(8,128)(2,1)}, f32[8,1152]{1,0:T(8,128)}) custom-call(s32[3]{0:T(128)} %add_add_fusion.scalars_ref, bf16[768,1152]{1,0:T(8,128)(2,1)} %get-tuple-element.70.q_ref.kn_ref.vn_ref, bf16[768,1152]{1,0:T(8,128)(2,1)} %get-tuple-element.70.q_ref.kn_ref.vn_ref, ...), custom_call_target="tpu_custom_call" | custom-call | flops 1 | bytes 1 | tf_op jit(solution)/shard_map/attend_back/pallas_call | solution.py:370
  194.0 2.3 convolution_convert_fusion.3
  202.3 3.2 collective-permute-done.25
  214.4 18.5 %attend_back.3 = (bf16[1536,768]{1,0:T(8,128)(2,1)}, bf16[384,1152]{1,0:T(8,128)(2,1)}, f32[8,1152]{1,0:T(8,128)}) custom-call(s32[3]{0:T(128)} %add_add_fusion.1.scalars_ref, bf16[768,1152]{1,0:T(8,128)(2,1)} %get-tuple-element.70.q_ref.kn_ref.vn_ref, bf16[768,1152]{1,0:T(8,128)(2,1)} %get-tuple-element.70.q_ref.kn_ref.vn_ref, ...), custom_call_target="tpu_custom_call" | custom-call | flops 1 | bytes 1 | tf_op jit(solution)/shard_map/attend_back/pallas_call | solution.py:370
  234.9 2.3 convolution_convert_fusion.2
  246.4 2.1 convolution_add_fusion.1
  264.3 9.2 %collective-permute-done.33 = bf16[4,104,768]{2,1,0:T(8,128)(2,1)S(1)} collective-permute-done((bf16[4,104,768]{2,1,0:T(8,128)(2,1)S(1)}, bf16[4,104,768]{2,1,0:T(8,128)(2,1)S(1)}, u32[]{:S(2)}, u32[]{:S(2)}) %collective-permute-start.33) | collective-permute-done | bytes 639008 | tf_op jit(solution)/shard_map/ppermute | solution.py:601
  273.7 2.3 collective-permute-start.34
  279.7 3.1 collective-permute-done.34
  282.9 6.1 %collective-permute-done.36 = bf16[104,768]{1,0:T(8,128)(2,1)S(1)} collective-permute-done((bf16[104,768]{1,0:T(8,128)(2,1)S(1)}, bf16[104,768]{1,0:T(8,128)(2,1)S(1)}, u32[]{:S(2)}, u32[]{:S(2)}) %collective-permute-start.36) | collective-permute-done | bytes 159776 | tf_op jit(solution)/shard_map/ppermute | solution.py:608
  289.0 11.6 %collective-permute-done.35 = bf16[104,768]{1,0:T(8,128)(2,1)S(1)} collective-permute-done((bf16[104,768]{1,0:T(8,128)(2,1)S(1)}, bf16[104,768]{1,0:T(8,128)(2,1)S(1)}, u32[]{:S(2)}, u32[]{:S(2)}) %collective-permute-start.35) | collective-permute-done | bytes 159776 | tf_op jit(solution)/shard_map/ppermute | solution.py:608
  306.8 2.5 fusion.14
  309.4 17.4 %reduce-scatter.4.cloned.1.call-done = bf16[24,6272]{1,0:T(8,128)(2,1)} async-done(((bf16[768,6272]{1,0:T(8,128)(2,1)}), bf16[24,6272]{1,0:T(8,128)(2,1)}) %reduce-scatter.4.cloned.1.call-update) | async-done | bytes 301072
  336.0 2.6 reshape.325
  338.5 2.3 collective-permute-done.38
  342.3 3.6 collective-permute-start.41
  348.8 4.6 %collective-permute-done.40 = bf16[48,1152]{1,0:T(8,128)(2,1)S(1)} collective-permute-done((bf16[48,1152]{1,0:T(8,128)(2,1)S(1)}, bf16[48,1152]{1,0:T(8,128)(2,1)S(1)}, u32[]{:S(2)}, u32[]{:S(2)}) %collective-permute-start.40) | collective-permute-done | bytes 110624 | tf_op jit(solution)/shard_map/ppermute | solution.py:608
  (379 shorter events, 123.4 us)
Async XLA Ops:
  7.3 141.2 %all-gather.2.cloned.1.call-start = ((), (), s32[]{:S(2)}) async-start(), calls=%async_computation.1 | async-start | bytes 11151360 | tf_op jit(solution)/shard_map/all_gather | solution.py:744
  9.9 27.0 %collective-permute-start = (bf16[2,2,96,768]{3,2,1,0:T(8,128)(2,1)}, bf16[2,2,96,768]{3,2,1,0:T(8,128)(2,1)S(1)}, u32[]{:S(2)}, u32[]{:S(2)}) collective-permute-start(bf16[2,2,96,768]{3,2,1,0:T(8,128)(2,1)} %param.16), channel_id=1, source_target_pairs={{0,1},{1,0},{2,3},{3,2},{4,5},{5,4},{6,7},{7,6},{8,9},{9,8},{10,11... | collective-permute-start | bytes 1769480 | tf_op jit(solution)/shard_map/ppermute | solution.py:598
  21.3 10.8 %collective-permute-start.4 = (bf16[48,1152]{1,0:T(8,128)(2,1)}, bf16[48,1152]{1,0:T(8,128)(2,1)S(1)}, u32[]{:S(2)}, u32[]{:S(2)}) collective-permute-start(bf16[48,1152]{1,0:T(8,128)(2,1)} %bitcast.143), channel_id=1, source_target_pairs={{0,8},{1,9},{2,10},{3,11},{4,12},{5,13},{6,14},{7,15},{8,0},{9,1},... | collective-permute-start | bytes 331784 | tf_op jit(solution)/shard_map/ppermute | solution.py:608
  21.3 10.8 %collective-permute-start.3 = (bf16[48,1152]{1,0:T(8,128)(2,1)}, bf16[48,1152]{1,0:T(8,128)(2,1)S(1)}, u32[]{:S(2)}, u32[]{:S(2)}) collective-permute-start(bf16[48,1152]{1,0:T(8,128)(2,1)} %bitcast.143), channel_id=1, source_target_pairs={{0,4},{1,5},{2,6},{3,7},{4,8},{5,9},{6,10},{7,11},{8,12},{9,13},{1... | collective-permute-start | bytes 331784 | tf_op jit(solution)/shard_map/ppermute | solution.py:608
  33.9 12.0 %collective-permute-start.10 = (bf16[4,48,1152]{2,1,0:T(8,128)(2,1)S(1)}, bf16[4,48,1152]{2,1,0:T(8,128)(2,1)}, u32[]{:S(2)}, u32[]{:S(2)}) collective-permute-start(bf16[4,48,1152]{2,1,0:T(8,128)(2,1)S(1)} %pad_maximum_fusion.7.refs_0_), channel_id=1, source_target_pairs={{0,16},{16,0},{1,17},{17,1},{2,18},{18,2},{3,19},{19,3},{4,20},{20... | collective-permute-start | bytes 1327112 | tf_op jit(solution)/shard_map/ppermute | solution.py:604
  35.5 11.6 %collective-permute-start.9 = (bf16[4,48,1152]{2,1,0:T(8,128)(2,1)S(1)}, bf16[4,48,1152]{2,1,0:T(8,128)(2,1)}, u32[]{:S(2)}, u32[]{:S(2)}) collective-permute-start(bf16[4,48,1152]{2,1,0:T(8,128)(2,1)S(1)} %pad_maximum_fusion.7.refs_0_), channel_id=1, source_target_pairs={{0,2},{1,3},{2,0},{3,1},{4,6},{5,7},{6,4},{7,5},{8,10},{9,11},{10,... | collective-permute-start | bytes 1327112 | tf_op jit(solution)/shard_map/ppermute | solution.py:601
  37.0 10.1 %collective-permute-start.8 = (bf16[104,768]{1,0:T(8,128)(2,1)S(1)}, bf16[104,768]{1,0:T(8,128)(2,1)}, u32[]{:S(2)}, u32[]{:S(2)}) collective-permute-start(bf16[104,768]{1,0:T(8,128)(2,1)S(1)} %fusion.56), channel_id=1, source_target_pairs={{0,12},{1,13},{2,14},{3,15},{4,0},{5,1},{6,2},{7,3},{8,4},{9,5},{1... | collective-permute-start | bytes 479240 | tf_op jit(solution)/shard_map/ppermute | solution.py:608
  38.4 14.1 %collective-permute-start.7 = (bf16[104,768]{1,0:T(8,128)(2,1)S(1)}, bf16[104,768]{1,0:T(8,128)(2,1)}, u32[]{:S(2)}, u32[]{:S(2)}) collective-permute-start(bf16[104,768]{1,0:T(8,128)(2,1)S(1)} %fusion.56), channel_id=1, source_target_pairs={{0,8},{1,9},{2,10},{3,11},{4,12},{5,13},{6,14},{7,15},{8,0},{9,1},... | collective-permute-start | bytes 479240 | tf_op jit(solution)/shard_map/ppermute | solution.py:608
  39.1 13.4 %collective-permute-start.6 = (bf16[104,768]{1,0:T(8,128)(2,1)S(1)}, bf16[104,768]{1,0:T(8,128)(2,1)}, u32[]{:S(2)}, u32[]{:S(2)}) collective-permute-start(bf16[104,768]{1,0:T(8,128)(2,1)S(1)} %fusion.56), channel_id=1, source_target_pairs={{0,4},{1,5},{2,6},{3,7},{4,8},{5,9},{6,10},{7,11},{8,12},{9,13},{1... | collective-permute-start | bytes 479240 | tf_op jit(solution)/shard_map/ppermute | solution.py:608
  52.5 274.3 %reduce-scatter.4.cloned.1.call-start = ((), (), s32[]{:S(2)}) async-start(), calls=%async_computation.2 | async-start | bytes 9934848
  53.8 16.7 %collective-permute-start.11 = (bf16[4,104,768]{2,1,0:T(8,128)(2,1)S(1)}, bf16[4,104,768]{2,1,0:T(8,128)(2,1)}, u32[]{:S(2)}, u32[]{:S(2)}) collective-permute-start(bf16[4,104,768]{2,1,0:T(8,128)(2,1)S(1)} %pad_maximum_fusion.4.a_ref), channel_id=1, source_target_pairs={{0,2},{1,3},{2,0},{3,1},{4,6},{5,7},{6,4},{7,5},{8,10},{9,11},{10,... | collective-permute-start | bytes 1916936 | tf_op jit(solution)/shard_map/ppermute | solution.py:601
  55.0 16.4 %collective-permute-start.14 = (bf16[96,768]{1,0:T(8,128)(2,1)S(1)}, bf16[96,768]{1,0:T(8,128)(2,1)S(1)}, u32[]{:S(2)}, u32[]{:S(2)}) collective-permute-start(bf16[96,768]{1,0:T(8,128)(2,1)S(1)} %get-tuple-element.67), channel_id=1, source_target_pairs={{0,12},{1,13},{2,14},{3,15},{4,0},{5,1},{6,2},{7,3},{8,4},{9,5},{1... | collective-permute-start | bytes 442376 | tf_op jit(solution)/shard_map/ppermute | solution.py:608
  55.1 21.1 %collective-permute-start.13 = (bf16[96,768]{1,0:T(8,128)(2,1)S(1)}, bf16[96,768]{1,0:T(8,128)(2,1)S(1)}, u32[]{:S(2)}, u32[]{:S(2)}) collective-permute-start(bf16[96,768]{1,0:T(8,128)(2,1)S(1)} %get-tuple-element.67), channel_id=1, source_target_pairs={{0,8},{1,9},{2,10},{3,11},{4,12},{5,13},{6,14},{7,15},{8,0},{9,1},... | collective-permute-start | bytes 442376 | tf_op jit(solution)/shard_map/ppermute | solution.py:608
  56.4 19.8 %collective-permute-start.12 = (bf16[96,768]{1,0:T(8,128)(2,1)S(1)}, bf16[96,768]{1,0:T(8,128)(2,1)S(1)}, u32[]{:S(2)}, u32[]{:S(2)}) collective-permute-start(bf16[96,768]{1,0:T(8,128)(2,1)S(1)} %get-tuple-element.67), channel_id=1, source_target_pairs={{0,4},{1,5},{2,6},{3,7},{4,8},{5,9},{6,10},{7,11},{8,12},{9,13},{1... | collective-permute-start | bytes 442376 | tf_op jit(solution)/shard_map/ppermute | solution.py:608
  58.5 19.2 %collective-permute-start.16 = (bf16[4,48,1152]{2,1,0:T(8,128)(2,1)}, bf16[4,48,1152]{2,1,0:T(8,128)(2,1)S(1)}, u32[]{:S(2)}, u32[]{:S(2)}) collective-permute-start(bf16[4,48,1152]{2,1,0:T(8,128)(2,1)} %collective-permute-done.9.refs_1_), channel_id=1, source_target_pairs={{0,16},{16,0},{1,17},{17,1},{2,18},{18,2},{3,19},{19,3},{4,20},{20... | collective-permute-start | bytes 1327112 | tf_op jit(solution)/shard_map/ppermute | solution.py:604
  77.7 16.1 %collective-permute-start.17 = (bf16[4,104,768]{2,1,0:T(8,128)(2,1)S(1)}, bf16[4,104,768]{2,1,0:T(8,128)(2,1)S(1)}, u32[]{:S(2)}, u32[]{:S(2)}) collective-permute-start(bf16[4,104,768]{2,1,0:T(8,128)(2,1)S(1)} %pad_maximum_fusion.4.a_ref), channel_id=1, source_target_pairs={{0,1},{1,0},{2,3},{3,2},{4,5},{5,4},{6,7},{7,6},{8,9},{9,8},{10,11... | collective-permute-start | bytes 1916936 | tf_op jit(solution)/shard_map/ppermute | solution.py:598
  91.6 15.3 %collective-permute-start.19 = (bf16[4,96,768]{2,1,0:T(8,128)(2,1)S(1)}, bf16[4,96,768]{2,1,0:T(8,128)(2,1)S(1)}, u32[]{:S(2)}, u32[]{:S(2)}) collective-permute-start(bf16[4,96,768]{2,1,0:T(8,128)(2,1)S(1)} %pad_maximum_fusion.5.a_ref), channel_id=1, source_target_pairs={{0,2},{1,3},{2,0},{3,1},{4,6},{5,7},{6,4},{7,5},{8,10},{9,11},{10,... | collective-permute-start | bytes 1769480 | tf_op jit(solution)/shard_map/ppermute | solution.py:601
  93.8 28.4 %collective-permute-start.20 = (bf16[4,96,768]{2,1,0:T(8,128)(2,1)S(1)}, bf16[4,96,768]{2,1,0:T(8,128)(2,1)S(1)}, u32[]{:S(2)}, u32[]{:S(2)}) collective-permute-start(bf16[4,96,768]{2,1,0:T(8,128)(2,1)S(1)} %pad_maximum_fusion.5.a_ref), channel_id=1, source_target_pairs={{0,1},{1,0},{2,3},{3,2},{4,5},{5,4},{6,7},{7,6},{8,9},{9,8},{10,11... | collective-permute-start | bytes 1769480 | tf_op jit(solution)/shard_map/ppermute | solution.py:598
  106.9 15.3 %collective-permute-start.21 = (bf16[4,96,768]{2,1,0:T(8,128)(2,1)S(1)}, bf16[4,96,768]{2,1,0:T(8,128)(2,1)S(1)}, u32[]{:S(2)}, u32[]{:S(2)}) collective-permute-start(bf16[4,96,768]{2,1,0:T(8,128)(2,1)S(1)} %collective-permute-done.19.b_ref), channel_id=1, source_target_pairs={{0,1},{1,0},{2,3},{3,2},{4,5},{5,4},{6,7},{7,6},{8,9},{9,8},{10,11... | collective-permute-start | bytes 1769480 | tf_op jit(solution)/shard_map/ppermute | solution.py:598
  207.3 25.7 %collective-permute-start.26 = (bf16[4,2,24,768]{3,2,0,1:T(8,128)(2,1)S(1)}, bf16[4,2,24,768]{3,2,0,1:T(8,128)(2,1)S(1)}, u32[]{:S(2)}, u32[]{:S(2)}) collective-permute-start(bf16[4,2,24,768]{3,2,0,1:T(8,128)(2,1)S(1)} %bitcast.310), channel_id=1, source_target_pairs={{0,16},{16,0},{1,17},{17,1},{2,18},{18,2},{3,19},{19,3},{4,20},{20... | collective-permute-start | bytes 884744 | tf_op jit(solution)/shard_map/ppermute | solution.py:604
  212.9 46.1 %collective-permute-start.27 = (bf16[4,96,768]{2,1,0:T(8,128)(2,1)}, bf16[4,96,768]{2,1,0:T(8,128)(2,1)}, u32[]{:S(2)}, u32[]{:S(2)}) collective-permute-start(bf16[4,96,768]{2,1,0:T(8,128)(2,1)} %dynamic-slice_bitcast_fusion.2), channel_id=1, source_target_pairs={{0,2},{1,3},{2,0},{3,1},{4,6},{5,7},{6,4},{7,5},{8,10},{9,11},{10,... | collective-permute-start | bytes 1769480 | tf_op jit(solution)/shard_map/ppermute | solution.py:601
  234.4 23.6 %collective-permute-start.28 = (bf16[4,24,768]{2,1,0:T(8,128)(2,1)}, bf16[4,24,768]{2,1,0:T(8,128)(2,1)}, u32[]{:S(2)}, u32[]{:S(2)}) collective-permute-start(bf16[4,24,768]{2,1,0:T(8,128)(2,1)} %dynamic-slice_bitcast_fusion.9), channel_id=1, source_target_pairs={{0,2},{1,3},{2,0},{3,1},{4,6},{5,7},{6,4},{7,5},{8,10},{9,11},{10,... | collective-permute-start | bytes 442376 | tf_op jit(solution)/shard_map/ppermute | solution.py:601
  241.3 13.3 %collective-permute-start.32 = (bf16[10,96,768]{2,1,0:T(8,128)(2,1)}, bf16[10,96,768]{2,1,0:T(8,128)(2,1)}, u32[]{:S(2)}, u32[]{:S(2)}) collective-permute-start(bf16[10,96,768]{2,1,0:T(8,128)(2,1)} %pad_maximum_fusion.1), channel_id=1, source_target_pairs={{0,1},{1,0},{2,3},{3,2},{4,5},{5,4},{6,7},{7,6},{8,9},{9,8},{10,11... | collective-permute-start | bytes 4423688 | tf_op jit(solution)/shard_map/ppermute | solution.py:598
  251.0 75.8 %collective-permute-start.37 = (bf16[4,2,48,1152]{3,2,0,1:T(8,128)(2,1)}, bf16[4,2,48,1152]{3,2,0,1:T(8,128)(2,1)}, u32[]{:S(2)}, u32[]{:S(2)}) collective-permute-start(bf16[4,2,48,1152]{3,2,0,1:T(8,128)(2,1)} %copy_bitcast_fusion), channel_id=1, source_target_pairs={{0,16},{16,0},{1,17},{17,1},{2,18},{18,2},{3,19},{19,3},{4,20},{20... | collective-permute-start | bytes 2654216 | tf_op jit(solution)/shard_map/ppermute | solution.py:604
  256.7 16.9 %collective-permute-start.33 = (bf16[4,104,768]{2,1,0:T(8,128)(2,1)S(1)}, bf16[4,104,768]{2,1,0:T(8,128)(2,1)S(1)}, u32[]{:S(2)}, u32[]{:S(2)}) collective-permute-start(bf16[4,104,768]{2,1,0:T(8,128)(2,1)S(1)} %fusion.23), channel_id=1, source_target_pairs={{0,2},{1,3},{2,0},{3,1},{4,6},{5,7},{6,4},{7,5},{8,10},{9,11},{10,... | collective-permute-start | bytes 1916936 | tf_op jit(solution)/shard_map/ppermute | solution.py:601
  260.4 15.6 %collective-permute-start.31 = (bf16[120,768]{1,0:T(8,128)(2,1)S(1)}, bf16[120,768]{1,0:T(8,128)(2,1)S(1)}, u32[]{:S(2)}, u32[]{:S(2)}) collective-permute-start(bf16[120,768]{1,0:T(8,128)(2,1)S(1)} %get-tuple-element.125), channel_id=1, source_target_pairs={{0,12},{1,13},{2,14},{3,15},{4,0},{5,1},{6,2},{7,3},{8,4},{9,5},{1... | collective-permute-start | bytes 552968 | tf_op jit(solution)/shard_map/ppermute | solution.py:608
  260.4 17.4 %collective-permute-start.29 = (bf16[120,768]{1,0:T(8,128)(2,1)S(1)}, bf16[120,768]{1,0:T(8,128)(2,1)S(1)}, u32[]{:S(2)}, u32[]{:S(2)}) collective-permute-start(bf16[120,768]{1,0:T(8,128)(2,1)S(1)} %get-tuple-element.126), channel_id=1, source_target_pairs={{0,4},{1,5},{2,6},{3,7},{4,8},{5,9},{6,10},{7,11},{8,12},{9,13},{1... | collective-permute-start | bytes 552968 | tf_op jit(solution)/shard_map/ppermute | solution.py:608
  262.4 15.4 %collective-permute-start.30 = (bf16[120,768]{1,0:T(8,128)(2,1)S(1)}, bf16[120,768]{1,0:T(8,128)(2,1)S(1)}, u32[]{:S(2)}, u32[]{:S(2)}) collective-permute-start(bf16[120,768]{1,0:T(8,128)(2,1)S(1)} %get-tuple-element.127), channel_id=1, source_target_pairs={{0,8},{1,9},{2,10},{3,11},{4,12},{5,13},{6,14},{7,15},{8,0},{9,1},... | collective-permute-start | bytes 552968 | tf_op jit(solution)/shard_map/ppermute | solution.py:608
  273.7 9.1 %collective-permute-start.34 = (bf16[104,768]{1,0:T(8,128)(2,1)S(1)}, bf16[104,768]{1,0:T(8,128)(2,1)S(1)}, u32[]{:S(2)}, u32[]{:S(2)}) collective-permute-start(bf16[104,768]{1,0:T(8,128)(2,1)S(1)} %get-tuple-element.128), channel_id=1, source_target_pairs={{0,4},{1,5},{2,6},{3,7},{4,8},{5,9},{6,10},{7,11},{8,12},{9,13},{1... | collective-permute-start | bytes 479240 | tf_op jit(solution)/shard_map/ppermute | solution.py:608
  276.0 13.0 %collective-permute-start.36 = (bf16[104,768]{1,0:T(8,128)(2,1)S(1)}, bf16[104,768]{1,0:T(8,128)(2,1)S(1)}, u32[]{:S(2)}, u32[]{:S(2)}) collective-permute-start(bf16[104,768]{1,0:T(8,128)(2,1)S(1)} %get-tuple-element.129), channel_id=1, source_target_pairs={{0,12},{1,13},{2,14},{3,15},{4,0},{5,1},{6,2},{7,3},{8,4},{9,5},{1... | collective-permute-start | bytes 479240 | tf_op jit(solution)/shard_map/ppermute | solution.py:608
  277.8 22.8 %collective-permute-start.35 = (bf16[104,768]{1,0:T(8,128)(2,1)S(1)}, bf16[104,768]{1,0:T(8,128)(2,1)S(1)}, u32[]{:S(2)}, u32[]{:S(2)}) collective-permute-start(bf16[104,768]{1,0:T(8,128)(2,1)S(1)} %get-tuple-element.130), channel_id=1, source_target_pairs={{0,8},{1,9},{2,10},{3,11},{4,12},{5,13},{6,14},{7,15},{8,0},{9,1},... | collective-permute-start | bytes 479240 | tf_op jit(solution)/shard_map/ppermute | solution.py:608
  329.9 10.9 %collective-permute-start.38 = (bf16[4,48,1152]{2,1,0:T(8,128)(2,1)}, bf16[4,48,1152]{2,1,0:T(8,128)(2,1)}, u32[]{:S(2)}, u32[]{:S(2)}) collective-permute-start(bf16[4,48,1152]{2,1,0:T(8,128)(2,1)} %dynamic-slice_bitcast_fusion.3), channel_id=1, source_target_pairs={{0,2},{1,3},{2,0},{3,1},{4,6},{5,7},{6,4},{7,5},{8,10},{9,11},{10,... | collective-permute-start | bytes 1327112 | tf_op jit(solution)/shard_map/ppermute | solution.py:601
  (84 other events, 488.5 us)
Sparse Core Ops, SparseCore 0:
  52.6 91.7 all-gather.1
  172.6 154.1 reduce-scatter.3
